TPU v7x, 128 devices: a whole 4x4x4 slice. The times are simulated.
128 devices in a mesh: row: 4 (over x), col: 32 (over z, y, core).
Axes of the slice: x: 4, y: 4, z: 4, core: 2. Of those that a mesh axis runs over, the one named last changes fastest.
Arguments:
- flexibility: float32 [4, 32, 5, 1024, 1024], P('row', 'col'), as said below
- coupling: float32 [4, 32, 5, 24, 1024], P('row', 'col'), may hold values from -0.75 to 0.75
- coarse_inverse: float32 [6144, 6144], P(('row', 'col')), as said below
- precon_weight: float32 [4, 32, 5, 4, 128], P('row', 'col'), may hold values from 0.25 to 2
- right_side: float32 [4, 32, 5, 16, 4, 128], P('row', 'col'), may hold values from -6 to 6
- counts: int32 [4, 32], P('row', 'col'), may hold values from 2 to 5, as said below
- partner: int32 [4, 32, 4, 5], P('row', 'col'), may hold values from 0 to 4, each once within a row
- dof_index: int32 [4, 32, 5, 4, 128], P('row', 'col'), may hold values from 0 to 127, each once within a row
- corner_map: int32 [4, 32, 5, 24], P('row', 'col'), may hold values from 0 to 6143
Outputs:
- solution: float32 [4, 32, 5, 16, 4, 128], P('row', 'col')
- residual: float32 [4, 32, 5, 16, 4, 128], P('row', 'col')
Inputs may be any that keep to these rules, and one draw needn't show every extreme that they name: A device's live subdomains are its first counts slots; some device has 5 and some device has 2 in every draw. `partner`: for each device and each link block separately, the 5 entries are a permutation of the slots; the same values recur on other devices, link blocks and device rows. `dof_index`: for each device, slot and link block separately, the 128 entries are a permutation of the block's unknowns; the same values recur on other slots, link blocks, devices and device rows. `flexibility`: symmetric positive definite. `coarse_inverse`: symmetric positive definite.
All inputs are finite; a program needn't handle non-finite values.
Results may differ from a plain program's by a relative error of at most 0.00029.
Values sent between devices are 32-bit elements; how exact they have to be, the bound alone decides.
A program may use at most 128 MiB of HBM per device.

v0:
```python
import jax
import jax.numpy as jnp
from jax import lax
from jax.sharding import PartitionSpec as P

ITERS = 3


HIGH = lax.Precision.HIGHEST


def shifted(x, axis, by):
    devices = lax.axis_size(axis)
    return lax.ppermute(x, axis, [(i, (i + by) % devices) for i in range(devices)])


def local(
    flexibility,
    coupling,
    coarse_inverse,
    precon_weight,
    right_side,
    counts,
    partner,
    dof_index,
    corner_map,
):
    flex_local = flexibility[0, 0]
    coupling_local = coupling[0, 0]
    slots = flex_local.shape[0]
    iface = flex_local.shape[1]
    links = partner.shape[2]
    width = dof_index.shape[-1]
    loads = right_side.shape[3]
    corners = corner_map.shape[-1]
    coarse_size = coarse_inverse.shape[1]
    slot_ids = jnp.arange(slots, dtype=jnp.int32)
    counts_prev = shifted(counts, "col", 1)
    partner_next = shifted(partner, "col", -1)
    live = (slot_ids < counts[0, 0]).astype(jnp.float32)
    live_prev = (slot_ids < counts_prev[0, 0]).astype(jnp.float32)
    chosen_own = (partner[0, 0][..., None] == slot_ids).astype(jnp.float32)
    chosen_next = (partner_next[0, 0][..., None] == slot_ids).astype(jnp.float32)
    link_live = jnp.einsum("kjp,p->jk", chosen_own, live_prev, precision=HIGH)
    mask_links = (live[:, None] * link_live)[:, None, :, None]
    permuter = (dof_index[0, 0][..., None] == jnp.arange(width, dtype=jnp.int32)).astype(
        jnp.float32
    )
    corner_table = (
        corner_map[0, 0].reshape(-1)[:, None] == jnp.arange(coarse_size, dtype=jnp.int32)
    ).astype(jnp.float32)

    def local_inner(first, second):
        return jnp.sum(first * second, axis=(0, 2, 3))

    def broadcast_loads(scalars):
        return scalars[None, :, None, None]

    weight = precon_weight[0, 0][:, None]
    residual = right_side[0, 0] * mask_links
    solution = jnp.zeros_like(residual)

    def precond_norm(resid_now, precond_now):
        return lax.psum(local_inner(resid_now, precond_now), ("row", "col"))

    precond = weight * residual
    direction = precond
    norm_now = precond_norm(residual, precond)
    for iteration in range(ITERS):
        forces = jnp.einsum("jkmi,jqkm->jqki", permuter, direction, precision=HIGH)
        forces_next = shifted(forces, "col", -1)
        facing = -jnp.einsum("kjp,jqkw->pqkw", chosen_next, forces_next, precision=HIGH)
        force_full = jnp.concatenate([direction, facing], axis=2).reshape(slots, loads, iface)
        answer = jnp.einsum("sab,sqb->sqa", flex_local, force_full, precision=HIGH)
        corner_terms = jnp.einsum(
            "snb,sqb->qsn", coupling_local, force_full, precision=HIGH
        ).reshape(loads, slots * corners)
        apply_local_load = jnp.dot(
            corner_terms, corner_table, precision=HIGH, preferred_element_type=jnp.float32
        )
        total_load = lax.psum(apply_local_load, ("row", "col"))
        own_rows = lax.dot_general(
            total_load,
            coarse_inverse,
            (((1,), (1,)), ((), ())),
            precision=HIGH,
            preferred_element_type=jnp.float32,
        )
        corner_answer = lax.all_gather(own_rows, ("row", "col"), axis=1, tiled=True)
        picked = lax.dot_general(
            corner_answer,
            corner_table,
            (((1,), (1,)), ((), ())),
            precision=HIGH,
            preferred_element_type=jnp.float32,
        )
        picked = picked.reshape(loads, slots, corners)
        answer = answer + jnp.einsum("snb,qsn->sqb", coupling_local, picked, precision=HIGH)
        split = answer.reshape(slots, loads, 2 * links, width)
        link_part = split[:, :, :links, :]
        facing_prev = shifted(split[:, :, links:, :], "col", 1)
        selected = jnp.einsum("kjp,pqkw->jqkw", chosen_own, facing_prev, precision=HIGH)
        selected = jnp.einsum("jkmi,jqki->jqkm", permuter, selected, precision=HIGH)
        image = (link_part - selected) * mask_links
        curvature = lax.psum(local_inner(direction, image), ("row", "col"))
        alpha = broadcast_loads(norm_now / curvature)
        solution = solution + alpha * direction
        residual = residual - alpha * image
        if iteration + 1 < ITERS:
            precond = weight * residual
            norm_next = precond_norm(residual, precond)
            direction = precond + broadcast_loads(norm_next / norm_now) * direction
            norm_now = norm_next
    return (solution[None, None], residual[None, None])


def solution(mesh):
    in_specs = (
        P("row", "col", None, None, None),
        P("row", "col", None, None, None),
        P(("row", "col"), None),
        P("row", "col", None, None, None),
        P("row", "col", None, None, None, None),
        P("row", "col"),
        P("row", "col", None, None),
        P("row", "col", None, None, None),
        P("row", "col", None, None),
    )
    out_specs = (P("row", "col", None, None, None, None), P("row", "col", None, None, None, None))
    return jax.shard_map(local, mesh=mesh, in_specs=in_specs, out_specs=out_specs, check_vma=False)
```

profile of v0, /device:TPU:1, one launch (start us, length us, event | category | flops | bytes accessed | tf_op | source)
XLA Modules:
  0.0 968.0 jit_solution(3415736418951578792)
XLA Ops:
  7.2 2.7 collective-permute-start
  10.7 0.7 copy.44
  11.4 1.6 fusion.64
  13.0 1.0 fusion.52
  14.0 1.8 fusion.27
  15.8 4.7 collective-permute-start.1
  21.5 2.3 collective-permute-done.2
  25.1 1.8 fusion.11
  27.1 20.0 %fusion.4 = f32[5,16,1024]{2,1,0:T(8,128)S(1)} fusion(f32[5,16,1024]{2,1,0:T(8,128)S(1)} %reshape.56, f32[1,1,5,1024,1024]{4,3,2,1,0:T(8,128)} %param.9), kind=kOutput, calls=%fused_computation.4 | convolution fusion | flops 1006632960 | bytes 21626880 | tf_op jit(solution)/shard_map/sab,sqb->sqa/dot_general | solution.py:74
  47.1 126.6 %all-reduce.5.cloned.1.call-done = f32[16,6144]{1,0:T(8,128)} async-done(((f32[16,6144]{1,0:T(8,128)}), f32[16,6144]{1,0:T(8,128)}) %all-reduce.5.cloned.1.call-update) | async-done | bytes 393232 | tf_op jit(solution)/shard_map/psum | solution.py:81
  173.6 2.0 convolution_bitcast_fusion.8
  175.7 36.1 %all-gather = f32[128,48,16]{1,2,0:T(8,128)S(1)} all-gather(f32[1,48,16]{1,2,0:T(8,128)S(1)} %convolution_bitcast_fusion.8), channel_id=1, replica_groups=mesh['row'=4,'col'=32] {'row','col'}, dimensions={0}, use_global_device_ids=true | all-gather | bytes 396288 | tf_op jit(solution)/shard_map/all_gather | solution.py:89
  212.2 1.4 reshape.69
  213.6 2.5 fusion.10
  217.1 3.3 collective-permute-done.3
  220.8 1.4 fusion.22
  222.6 67.4 %all-reduce = (f32[16]{0:T(128)S(1)}, f32[16]{0:T(128)S(1)}) all-reduce(f32[16]{0:T(128)S(1)} %get-tuple-element.9, f32[16]{0:T(128)S(1)} %get-tuple-element.8), channel_id=1, replica_groups=mesh['row'=4,'col'=32] {'row','col'}, use_global_device_ids=true, to_apply=%region_1.0 | all-reduce | flops 32 | bytes 256 | tf_op jit(solution)/shard_map/psum | solution.py:64
  290.5 62.5 %psum.66 = f32[16]{0:T(128)S(1)} all-reduce(f32[16]{0:T(128)S(1)} %get-tuple-element.14), channel_id=1, replica_groups=mesh['row'=4,'col'=32] {'row','col'}, use_global_device_ids=true, to_apply=%region_6.0 | all-reduce | flops 16 | bytes 128 | tf_op jit(solution)/shard_map/psum | solution.py:64
  353.1 1.1 fusion.28
  354.2 0.9 collective-permute-start.4
  355.0 4.3 collective-permute-done.4
  360.7 1.8 fusion.9
  362.6 20.6 %fusion.2 = f32[5,16,1024]{2,1,0:T(8,128)} fusion(f32[5,16,1024]{2,1,0:T(8,128)S(1)} %reshape.60, f32[1,1,5,1024,1024]{4,3,2,1,0:T(8,128)} %param.9), kind=kOutput, calls=%fused_computation.2 | convolution fusion | flops 1006632960 | bytes 21626880 | tf_op jit(solution)/shard_map/sab,sqb->sqa/dot_general | solution.py:74
  383.2 124.4 %all-reduce.7.cloned.1.call-done = f32[16,6144]{1,0:T(8,128)} async-done(((f32[16,6144]{1,0:T(8,128)}), f32[16,6144]{1,0:T(8,128)}) %all-reduce.7.cloned.1.call-update) | async-done | bytes 393232 | tf_op jit(solution)/shard_map/psum | solution.py:81
  507.5 2.0 convolution_bitcast_fusion.7
  509.5 35.9 %all-gather.1 = f32[128,48,16]{1,2,0:T(8,128)S(1)} all-gather(f32[1,48,16]{1,2,0:T(8,128)S(1)} %convolution_bitcast_fusion.7), channel_id=1, replica_groups=mesh['row'=4,'col'=32] {'row','col'}, dimensions={0}, use_global_device_ids=true | all-gather | bytes 396288 | tf_op jit(solution)/shard_map/all_gather | solution.py:89
  545.8 1.4 reshape.71
  547.2 2.5 fusion.8
  549.8 1.4 convolution_add_fusion.1
  552.2 3.3 collective-permute-done.5
  555.8 1.4 fusion.20
  557.5 67.4 %psum.68 = f32[16]{0:T(128)S(1)} all-reduce(f32[16]{0:T(128)S(1)} %multiply_reduce_fusion.1), channel_id=1, replica_groups=mesh['row'=4,'col'=32] {'row','col'}, use_global_device_ids=true, to_apply=%region_9.0 | all-reduce | flops 16 | bytes 128 | tf_op jit(solution)/shard_map/psum | solution.py:105
  625.3 62.5 %psum.69 = f32[16]{0:T(128)S(1)} all-reduce(f32[16]{0:T(128)S(1)} %get-tuple-element.12), channel_id=1, replica_groups=mesh['row'=4,'col'=32] {'row','col'}, use_global_device_ids=true, to_apply=%region_11.0 | all-reduce | flops 16 | bytes 128 | tf_op jit(solution)/shard_map/psum | solution.py:64
  687.9 1.1 fusion.29
  689.7 4.3 collective-permute-done.6
  695.3 1.8 fusion.7
  697.2 20.6 %fusion = f32[5,16,1024]{2,1,0:T(8,128)} fusion(f32[5,16,1024]{2,1,0:T(8,128)S(1)} %reshape.64, f32[1,1,5,1024,1024]{4,3,2,1,0:T(8,128)} %param.9), kind=kOutput, calls=%fused_computation | convolution fusion | flops 1006632960 | bytes 21626880 | tf_op jit(solution)/shard_map/sab,sqb->sqa/dot_general | solution.py:74
  717.8 124.4 %all-reduce.9.cloned.1.call-done = f32[16,6144]{1,0:T(8,128)} async-done(((f32[16,6144]{1,0:T(8,128)}), f32[16,6144]{1,0:T(8,128)}) %all-reduce.9.cloned.1.call-update) | async-done | bytes 393232 | tf_op jit(solution)/shard_map/psum | solution.py:81
  842.1 2.0 convolution_bitcast_fusion.6
  844.1 36.1 %all-gather.2 = f32[128,48,16]{1,2,0:T(8,128)S(1)} all-gather(f32[1,48,16]{1,2,0:T(8,128)S(1)} %convolution_bitcast_fusion.6), channel_id=1, replica_groups=mesh['row'=4,'col'=32] {'row','col'}, dimensions={0}, use_global_device_ids=true | all-gather | bytes 396288 | tf_op jit(solution)/shard_map/all_gather | solution.py:89
  880.6 1.4 reshape.73
  882.0 2.5 fusion.6
  884.6 1.4 convolution_add_fusion
  886.6 3.3 collective-permute-done.7
  890.2 1.4 fusion.18
  891.9 67.4 %psum.71 = f32[16]{0:T(128)S(1)} all-reduce(f32[16]{0:T(128)S(1)} %multiply_reduce_fusion), channel_id=1, replica_groups=mesh['row'=4,'col'=32] {'row','col'}, use_global_device_ids=true, to_apply=%region_14.0 | all-reduce | flops 16 | bytes 128 | tf_op jit(solution)/shard_map/psum | solution.py:105
  959.7 0.8 copy.76
  960.5 0.8 copy.75
  (84 shorter events, 12.7 us)
Async XLA Ops:
  7.2 166.5 %copy-start = (f32[48,6144]{1,0:T(8,128)S(1)}, f32[48,6144]{1,0:T(8,128)}, u32[]{:S(2)}) copy-start(f32[48,6144]{1,0:T(8,128)} %param.11) | copy-start | bytes 3538948
  7.2 17.3 %copy-start.1 = (f32[1,1,5,24,1024]{4,3,2,1,0:T(8,128)S(1)}, f32[1,1,5,24,1024]{4,3,2,1,0:T(8,128)}, u32[]{:S(2)}) copy-start(f32[1,1,5,24,1024]{4,3,2,1,0:T(8,128)} %param.10) | copy-start | bytes 1474564
  7.2 166.4 %all-reduce.5.cloned.1.call-start = ((), (), s32[]{:S(2)}) async-start(), calls=%async_computation | async-start | bytes 786432 | tf_op jit(solution)/shard_map/psum | solution.py:81
  7.2 4.2 collective-permute-start
  15.8 8.0 collective-permute-start.1
  20.6 3.2 collective-permute-start.2
  27.0 480.5 %all-reduce.7.cloned.1.call-start = ((), (), s32[]{:S(2)}) async-start(), calls=%async_computation.1 | async-start | bytes 786432 | tf_op jit(solution)/shard_map/psum | solution.py:81
  212.1 8.3 copy-start.5
  212.1 8.6 copy-start.6
  212.1 10.0 %copy-start.2 = (f32[1,1,5,16,4,128]{5,4,3,2,1,0:T(4,128)S(1)}, f32[1,1,5,16,4,128]{5,4,3,2,1,0:T(4,128)}, u32[]{:S(2)}) copy-start(f32[1,1,5,16,4,128]{5,4,3,2,1,0:T(4,128)} %param.13) | copy-start | bytes 491524
  216.8 3.6 collective-permute-start.3
  354.2 5.2 collective-permute-start.4
  362.5 479.6 %all-reduce.9.cloned.1.call-start = ((), (), s32[]{:S(2)}) async-start(), calls=%async_computation.2 | async-start | bytes 786432 | tf_op jit(solution)/shard_map/psum | solution.py:81
  551.5 4.0 collective-permute-start.5
  625.3 69.0 %copy-start.3 = (f32[5,16,4,128]{3,0,1,2:T(8,128)}, f32[5,16,4,128]{3,0,1,2:T(8,128)S(1)}, u32[]{:S(2)}) copy-start(f32[5,16,4,128]{3,0,1,2:T(8,128)S(1)} %get-tuple-element.13) | copy-start | bytes 491524
  689.0 5.0 collective-permute-start.6
  882.0 77.4 %copy-start.4 = (f32[5,16,4,128]{3,0,1,2:T(8,128)S(1)}, f32[5,16,4,128]{3,0,1,2:T(8,128)}, u32[]{:S(2)}) copy-start(f32[5,16,4,128]{3,0,1,2:T(8,128)} %copy-done.3) | copy-start | bytes 491524
  886.3 3.6 collective-permute-start.7
Sparse Core Ops, SparseCore 0:
  27.1 146.4 all-reduce.4
  362.7 144.8 all-reduce.6
  697.3 144.7 all-reduce.8
where the time goes:
time: 975 us; the launch traced here: 968 us
  blocking collectives  435 us (45%)
  waiting for transfers between devices  396 us (41%)
  matrix products  96.9 us (10%)
  between operations  15 us (2%)
  starting transfers between devices  10.6 us (1%)
    psum x3, waiting for transfers between devices, local(): total_load = lax.psum(apply_local_load, ('row', 'col'))  375 us
    psum x3, blocking collectives, precond_norm(): return lax.psum(local_inner(resid_now, precond_now), ('row', 'col'))  192 us
    psum x2, blocking collectives, local(): curvature = lax.psum(local_inner(direction, image), ('row', 'col'))  135 us
    all_gather x3, blocking collectives, local(): corner_answer = lax.all_gather(own_rows, ('row', 'col'), axis=1, tiled=True)  108 us
    dot_general x3, matrix products, local(): answer = jnp.einsum('sab,sqb->sqa', flex_local, force_full, precision=HIGH)  61.1 us
    ppermute x8, waiting for transfers between devices, shifted(): lax.ppermute(x, axis, [(i, (i + by) % devices) for i in range(devices)])  20.8 us
  transfers between devices with their start and end apart: 11, of which 9 were waited for; matrix products, arithmetic and copies ran while one was open for 6% of the time, Pallas kernels for 0%

commit v1 on v0

v1 whole, which is shorter than its diff:
```python
import functools

import jax
import jax.numpy as jnp
from jax import lax
from jax.experimental import pallas as pl
from jax.experimental.pallas import tpu as pltpu
from jax.sharding import PartitionSpec as P

ITERS = 3
NX, NZ, NY, NK = 4, 4, 4, 2
NYZ = NZ * NY
STAGES = 3
SCAL = 120

MESH = pl.DeviceIdType.MESH
F32 = jnp.float32
BF16 = jnp.bfloat16
NT = (((1,), (1,)), ((), ()))
NN = (((1,), (0,)), ((), ()))


def split2(value):
    high = value.astype(BF16)
    low = (value - high.astype(F32)).astype(BF16)
    return high, low


def split3(value):
    high = value.astype(BF16)
    rest = value - high.astype(F32)
    middle = rest.astype(BF16)
    low = (rest - middle.astype(F32)).astype(BF16)
    return high, middle, low


def stack3(value):
    return jnp.concatenate(split3(value), axis=0)


def dot(left, right, dims):
    return lax.dot_general(left, right, dims, preferred_element_type=F32)


def sum3(value):
    rows = value.shape[0] // 3
    return value[2 * rows :] + value[rows : 2 * rows] + value[:rows]


def rcopy(src, dst, send, recv, device):
    return pltpu.make_async_remote_copy(
        src_ref=src,
        dst_ref=dst,
        send_sem=send,
        recv_sem=recv,
        device_id=device,
        device_id_type=MESH,
    )


def group_start(src, buf, mine, send, recv, peers):
    for i, (device, _) in enumerate(peers):
        rcopy(src, buf.at[mine], send.at[i], recv.at[mine], device).start()


def group_wait(src, buf, send, recv, peers):
    for i, (device, theirs) in enumerate(peers):
        rcopy(src, buf.at[theirs], send.at[i], recv.at[theirs], device).wait_recv()
    for i, (device, theirs) in enumerate(peers):
        rcopy(src, buf.at[theirs], send.at[i], recv.at[theirs], device).wait_send()


def kernel(
    flex, cinv, cpl, weight, rhs, info, partner, partner_inv, dof, dof_inv,
    x_out, r_out,
    stage, flex_hi, flex_lo, m32, m_hi, m_lo, cplp, infop, maps, w32, wo_hi, wo_lo, wp_hi, wp_lo,
    scatter, pick, t8, ybuf, zbuf, cbuf, xbuf, abuf, gsend, frecv, usend, urecv,
    vblk, vsp, gsp, fsp, yv, tv, dv, sv, zv, rv, mask, ulink, clink, cface, sc, ans3,
    pxbuf, pcbuf, pybuf,
    flex_sem, mloc_sem, info_s, info_r, cpl_s, cpl_r, map_s, map_r, m_s, m_r,
    tx_s, tx_r, tc_s, tc_r, y_s, y_r, z_s, z_r, c_s, c_r, x_s, x_r, a_s, a_r,
    f_s, f_r, u_s, u_r, px_s, px_r, pc_s, pc_r, py_s, py_r,
):
    slots, iface = flex.shape[:2]
    half = iface // 2
    links, width = partner.shape[0], dof.shape[-1]
    loads = rhs.shape[1]
    corners = cpl.shape[1]
    own_rows, coarse = cinv.shape
    crange = coarse // NYZ
    cset = own_rows * NYZ
    blocks = slots * links
    tiles = 2 * width

    row, col = lax.axis_index("row"), lax.axis_index("col")
    cz = lax.div(col, NY * NK)
    cy = lax.rem(lax.div(col, NK), NY)
    ck = lax.rem(col, NK)
    cols = NZ * NY * NK
    me_yz = cz * NY + cy
    prev = (row, lax.rem(col + cols - 1, cols))
    nxt = (row, lax.rem(col + 1, cols))

    def device(x, z, y, k):
        return (x, (z * NY + y) * NK + k)

    def turn(value, by, size):
        return lax.rem(value + by, size)

    xs = [(turn(row, i, NX),) * 2 for i in (2, 1, 3)]
    xs = [(device(p, cz, cy, ck), p) for p, _ in xs]
    ys = [(device(row, cz, turn(cy, i, NY), ck), turn(cy, i, NY)) for i in (2, 1, 3)]
    zs = [(device(row, turn(cz, i, NZ), cy, ck), turn(cz, i, NZ)) for i in (2, 1, 3)]
    cs = [(device(row, cz, cy, 1 - ck), 1 - ck)]
    order = sorted(
        [(i, j) for i in range(NZ) for j in range(NY) if (i, j) != (0, 0)],
        key=lambda ij: -(min(ij[0], NZ - ij[0]) + min(ij[1], NY - ij[1])),
    )
    yzs = [
        (device(row, turn(cz, i, NZ), turn(cy, j, NY), ck), turn(cz, i, NZ) * NY + turn(cy, j, NY))
        for i, j in order
    ]
    xcs = [
        (device(turn(row, i, NX), cz, cy, turn(ck, j, NK)), turn(ck, j, NK) * NX + turn(row, i, NX))
        for i in range(NX)
        for j in range(NK)
        if (i, j) != (0, 0)
    ]
    me_xc = ck * NX + row

    def flex_copy(s):
        return pltpu.make_async_copy(flex.at[s], stage.at[s % STAGES], flex_sem.at[s])

    for s in range(STAGES):
        flex_copy(s).start()

    def m_part(other):
        return cinv.at[:, pl.ds(pl.multiple_of(other * crange, 128), crange)]

    m_local = pltpu.make_async_copy(m_part(me_yz), m32.at[me_yz], mloc_sem)
    m_local.start()

    barrier = pltpu.get_barrier_semaphore()
    everyone = [d for d, _ in yzs] + [d for d, _ in xcs] + [prev, nxt]
    for d in everyone:
        pl.semaphore_signal(barrier, inc=1, device_id=d, device_id_type=MESH)
    pl.semaphore_wait(barrier, len(everyone))

    info_copy = rcopy(info, infop, info_s, info_r, nxt)
    info_copy.start()
    for i, (d, _) in enumerate(xcs):
        rcopy(info.at[slots], maps.at[me_xc, 0], map_s.at[0, i], map_r.at[0, me_xc], d).start()
    cpl_copy = rcopy(cpl.at[:, :, half:], cplp, cpl_s, cpl_r, nxt)
    cpl_copy.start()
    for i, (d, other) in enumerate(yzs):
        rcopy(m_part(other), m32.at[me_yz], m_s.at[i], m_r.at[me_yz], d).start()

    def build_coupling(source, offset, out_hi, out_lo):
        w32[...] = jnp.zeros_like(w32)
        for s in range(slots):
            w32[s, s * corners : (s + 1) * corners, :] = source[s, :, offset : offset + half]
        for s in range(slots):
            high, low = split2(w32[s])
            out_hi[s] = high
            out_lo[s] = low

    build_coupling(cpl, 0, wo_hi, wo_lo)
    tv[...] = jnp.zeros_like(tv)
    dv[...] = jnp.zeros_like(dv)
    sv[...] = jnp.zeros_like(sv)
    x_out[...] = jnp.zeros_like(x_out)
    sc[0] = jnp.ones_like(sc[0])
    sc[1] = jnp.zeros_like(sc[1])
    sc[2] = jnp.zeros_like(sc[2])
    sc[3] = jnp.zeros_like(sc[3])

    info_copy.wait_recv()
    for i, (d, _) in enumerate(xcs):
        rcopy(infop.at[slots], maps.at[me_xc, 1], map_s.at[1, i], map_r.at[1, me_xc], d).start()
    maps[me_xc, 0] = info[slots]
    maps[me_xc, 1] = infop[slots]

    for b in range(blocks):
        s, k = b // links, b % links
        live = info[s] * infop[partner[k, s]]
        live = jnp.concatenate([live] * (loads // 8), axis=0)
        mask[b] = live
        resid = live * rhs[b]
        rv[b] = resid
        yv[b] = resid
        zv[b] = weight[b] * resid

    cpl_copy.wait_recv()
    build_coupling(cplp, 0, wp_hi, wp_lo)

    lane = lax.broadcasted_iota(jnp.int32, (loads, width), 1)

    def total(first, second):
        return jnp.sum(jnp.sum(first * second, axis=0), axis=1, keepdims=True)

    def scalar_terms():
        z, y = zv[...], yv[...]
        found = [total(rv[...], z), total(z, y), total(z, sv[...]), total(dv[...], y)]
        tile = jnp.zeros((loads, width), F32)
        for i, value in enumerate(found):
            tile = jnp.where(lane == SCAL + i, value, tile)
        return tile

    def update(tile, first):
        rz, zy, zs_, dy = [
            jnp.broadcast_to(
                jnp.sum(jnp.where(lane == SCAL + i, tile, 0.0), axis=1, keepdims=True), tile.shape
            )
            for i in range(4)
        ]
        beta = rz / sc[0]
        if first is not None:
            beta = jnp.where(first, 0.0, beta)
        curv = zy + beta * (zs_ + dy) + beta * beta * sc[1]
        alpha = rz / curv
        sc[0], sc[1], sc[2], sc[3] = rz, curv, alpha, beta
        direction = zv[...] + beta[None] * dv[...]
        image = yv[...] + beta[None] * sv[...]
        dv[...] = direction
        sv[...] = image
        x_out[...] = x_out[...] + alpha[None] * direction
        resid = rv[...] - alpha[None] * image
        rv[...] = resid
        return resid

    def put3(ref, s, k, value):
        for i, part in enumerate(split3(value)):
            ref[s, i * loads : (i + 1) * loads, k * width : (k + 1) * width] = part

    def take(value, index):
        index = jnp.broadcast_to(index, value.shape)
        return jnp.take_along_axis(value, index, axis=1, mode="promise_in_bounds")

    def convert(s):
        flex_copy(s).wait()
        here = s % STAGES

        def chunk(i, _):
            at = pl.ds(pl.multiple_of(i * 64, 64), 64)
            high, low = split2(stage[here, at, :])
            flex_hi[s, at, :] = high
            flex_lo[s, at, :] = low
            return 0

        lax.fori_loop(0, iface // 64, chunk, 0)
        if s + STAGES < slots:
            flex_copy(s + STAGES).start()

    def local_answers(it, first, last):
        @pl.when(it == 0)
        def _():
            for s in range(first, last):
                convert(s)

        def one(s, _):
            left = jnp.concatenate([vsp[s], fsp[s]], axis=1)
            for n in range(iface // 256):
                at = slice(n * 256, (n + 1) * 256)
                out = dot(left, flex_hi[s, :, at], NN) + dot(left, flex_lo[s, :, at], NN)
                out = sum3(out)
                for h in range(2):
                    piece = out[:, h * width : (h + 1) * width]
                    k = 2 * n + h
                    if k < links:
                        ulink[s * links + k] = piece
                    else:
                        usend[it, s * links + k - links] = piece
            return 0

        lax.fori_loop(first, last, one, 0)

    def body(it, _):
        tile = scalar_terms()
        for b in range(blocks):
            value = weight[b] * yv[b]
            vblk[b] = value
            put3(vsp, b // links, b % links, value)
        for b in range(blocks):
            p, k = b // links, b % links
            from_block = partner_inv[k, p] * links + k
            value = -take(vblk[from_block], dof_inv[from_block])
            gsend[it, b] = value
            put3(gsp, p, k, value)
        force_copy = rcopy(gsend.at[it], frecv.at[it], f_s.at[it], f_r.at[it], prev)
        force_copy.start()

        def terms(blocks3, high, low):
            found = None
            for s in range(slots):
                left = blocks3[s]
                part = dot(left, high[s], NT) + dot(left, low[s], NT)
                found = part if found is None else found + part
            return sum3(found)

        own = jnp.where(lane < SCAL, terms(vsp, wo_hi, wo_lo), tile)
        t8[it, ck, row, :, 0:width] = own
        t8[it, ck, row, :, width:tiles] = terms(gsp, wp_hi, wp_lo)
        group_start(t8.at[it, ck, row], t8.at[it, ck], row, tx_s.at[it], tx_r.at[it], xs)

        @pl.when(it == 0)
        def _():
            for source in range(2):
                for i, (d, other) in enumerate(xcs):
                    src = (info, infop)[source].at[slots]
                    cp = rcopy(
                        src, maps.at[other, source], map_s.at[source, i], map_r.at[source, other], d
                    )
                    cp.wait_recv()
                    cp.wait_send()

            def rows(b, _):
                base = (row * cols + b * NK + ck) * own_rows
                index = lax.broadcasted_iota(jnp.int32, (own_rows, width), 0) + base
                index = index.astype(F32)
                at = pl.ds(pl.multiple_of(b * own_rows, own_rows), own_rows)
                for q in range(NX * NK):
                    for h in range(2):
                        hit = jnp.where(index == maps[q, h, 0:1, :], 1.0, 0.0)
                        lo = (2 * q + h) * width
                        scatter[at, lo : lo + width] = hit.astype(BF16)
                return 0

            lax.fori_loop(0, NYZ, rows, 0)

        group_wait(t8.at[it, ck, row], t8.at[it, ck], tx_s.at[it], tx_r.at[it], xs)
        group_start(t8.at[it, ck], t8.at[it], ck, tc_s.at[it], tc_r.at[it], cs)
        group_wait(t8.at[it, ck], t8.at[it], tc_s.at[it], tc_r.at[it], cs)

        gathered = [t8[it, q // NX, q % NX] for q in range(NX * NK)]
        carried = gathered[0][:, :width]
        for value in gathered[1:]:
            carried = carried + value[:, :width]
        dense = sum3(dot(stack3(jnp.concatenate(gathered, axis=1)), scatter[...], NT))
        ybuf[it, cy, :, 0:cset] = dense
        ybuf[it, cy, :, cset : cset + width] = carried
        group_start(ybuf.at[it, cy], ybuf.at[it], cy, y_s.at[it], y_r.at[it], ys)

        force_copy.wait_recv()
        for b in range(blocks):
            put3(fsp, b // links, b % links, frecv[it, b])
        local_answers(it, 0, 2)

        group_wait(ybuf.at[it, cy], ybuf.at[it], y_s.at[it], y_r.at[it], ys)
        zbuf[it, cz] = ybuf[it, 0] + ybuf[it, 1] + ybuf[it, 2] + ybuf[it, 3]
        group_start(zbuf.at[it, cz], zbuf.at[it], cz, z_s.at[it], z_r.at[it], zs)

        local_answers(it, 2, 4)

        @pl.when(it == 0)
        def _():
            m_local.wait()
            for i, (d, other) in enumerate(yzs):
                cp = rcopy(m_part(other), m32.at[other], m_s.at[i], m_r.at[other], d)
                cp.wait_recv()
                cp.wait_send()
            for b in range(NYZ):
                high, low = split2(m32[b])
                m_hi[b * own_rows : (b + 1) * own_rows, :] = high
                m_lo[b * own_rows : (b + 1) * own_rows, :] = low

        group_wait(zbuf.at[it, cz], zbuf.at[it], z_s.at[it], z_r.at[it], zs)
        load = zbuf[it, 0] + zbuf[it, 1] + zbuf[it, 2] + zbuf[it, 3]
        scalars = load[:, cset:]
        left = stack3(load[:, :cset])
        cbuf[it, ck] = sum3(dot(left, m_hi[...], NN) + dot(left, m_lo[...], NN))
        group_start(cbuf.at[it, ck], cbuf.at[it], ck, c_s.at[it], c_r.at[it], cs)

        local_answers(it, 4, slots)
        answer_copy = rcopy(usend.at[it], urecv.at[it], u_s.at[it], u_r.at[it], nxt)
        answer_copy.start()

        group_wait(cbuf.at[it, ck], cbuf.at[it], c_s.at[it], c_r.at[it], cs)
        xbuf[it, row] = cbuf[it, 0] + cbuf[it, 1]
        group_start(xbuf.at[it, row], xbuf.at[it], row, x_s.at[it], x_r.at[it], xs)

        @pl.when(it > 0)
        def _():
            resid = update(scalars, it == 1)
            for b in range(blocks):
                zv[b] = weight[b] * resid[b]

        @pl.when(it == 0)
        def _():
            mine = [info[slots, 0:1, :], infop[slots, 0:1, :]]

            def rows(b, _):
                index = lax.broadcasted_iota(jnp.int32, (crange // 2, width), 0)
                index = (index + b * (crange // 2)).astype(F32)
                at = pl.ds(pl.multiple_of(b * (crange // 2), crange // 2), crange // 2)
                for h in range(2):
                    hit = jnp.where(index == mine[h], 1.0, 0.0)
                    pick[at, h * width : (h + 1) * width] = hit.astype(BF16)
                return 0

            lax.fori_loop(0, 2 * NYZ, rows, 0)

        group_wait(xbuf.at[it, row], xbuf.at[it], x_s.at[it], x_r.at[it], xs)
        abuf[it, me_yz] = xbuf[it, 0] + xbuf[it, 1] + xbuf[it, 2] + xbuf[it, 3]
        group_start(abuf.at[it, me_yz], abuf.at[it], me_yz, a_s.at[it], a_r.at[it], yzs)
        group_wait(abuf.at[it, me_yz], abuf.at[it], a_s.at[it], a_r.at[it], yzs)

        for b in range(NYZ):
            ans3[:, b * crange : (b + 1) * crange] = stack3(abuf[it, b])
        picked = stack3(sum3(dot(ans3[...], pick[...], NN)))
        for s in range(slots):
            found = dot(picked[:, :width], wo_hi[s], NN) + dot(picked[:, :width], wo_lo[s], NN)
            found = sum3(found)
            other = dot(picked[:, width:], wp_hi[s], NN) + dot(picked[:, width:], wp_lo[s], NN)
            other = sum3(other)
            for k in range(links):
                clink[s * links + k] = found[:, k * width : (k + 1) * width]
                cface[s * links + k] = other[:, k * width : (k + 1) * width]

        answer_copy.wait_recv()
        answer_copy.wait_send()
        force_copy.wait_send()
        alpha, beta = sc[2], sc[3]
        for b in range(blocks):
            s, k = b // links, b % links
            facing = partner[k, s] * links + k
            far = take(urecv[it, facing] + cface[facing], dof[b])
            image = (ulink[b] + clink[b] - far) * mask[b]
            image = image + beta * tv[b]
            tv[b] = jnp.where(it == 0, 0.0, image)
            yv[b] = jnp.where(it == 0, image, yv[b] - alpha * image)
        return 0

    lax.fori_loop(0, ITERS, body, 0)

    info_copy.wait_send()
    cpl_copy.wait_send()
    pxbuf[row] = scalar_terms()
    group_start(pxbuf.at[row], pxbuf, row, px_s, px_r, xs)
    group_wait(pxbuf.at[row], pxbuf, px_s, px_r, xs)
    pcbuf[ck] = pxbuf[0] + pxbuf[1] + pxbuf[2] + pxbuf[3]
    group_start(pcbuf.at[ck], pcbuf, ck, pc_s, pc_r, cs)
    group_wait(pcbuf.at[ck], pcbuf, pc_s, pc_r, cs)
    pybuf[me_yz] = pcbuf[0] + pcbuf[1]
    group_start(pybuf.at[me_yz], pybuf, me_yz, py_s, py_r, yzs)
    group_wait(pybuf.at[me_yz], pybuf, py_s, py_r, yzs)
    tile = pybuf[0]
    for b in range(1, NYZ):
        tile = tile + pybuf[b]
    r_out[...] = update(tile, None)


def local(
    flexibility,
    coupling,
    coarse_inverse,
    precon_weight,
    right_side,
    counts,
    partner,
    dof_index,
    corner_map,
):
    flex = flexibility[0, 0]
    cpl = coupling[0, 0]
    slots, iface = flex.shape[:2]
    half = iface // 2
    links, width = dof_index.shape[3:]
    loads = right_side.shape[3]
    own_rows, coarse = coarse_inverse.shape
    corners = corner_map.shape[-1]
    blocks = slots * links
    crange, cset = coarse // NYZ, own_rows * NYZ
    rows3 = 3 * loads

    weight = precon_weight[0, 0].reshape(blocks, 1, width)
    rhs = right_side[0, 0].transpose(0, 2, 1, 3).reshape(blocks, loads, width)
    slot_ids = jnp.arange(slots, dtype=jnp.int32)
    live = (slot_ids < counts[0, 0]).astype(F32)
    live = jnp.broadcast_to(live[:, None, None], (slots, 8, width))
    row_map = jnp.pad(
        corner_map[0, 0].reshape(-1).astype(F32), (0, width - slots * corners), constant_values=-1.0
    )
    info = jnp.concatenate([live, jnp.broadcast_to(row_map, (1, 8, width))], axis=0)
    own_partner = partner[0, 0]
    partner_inv = jnp.sum(
        jnp.where(own_partner[:, :, None] == slot_ids, slot_ids[None, :, None], 0), axis=1
    ).astype(jnp.int32)
    dof = dof_index[0, 0].reshape(blocks, 1, width)
    unknowns = jnp.arange(width, dtype=jnp.int32)
    dof_inv = jnp.sum(
        jnp.where(dof[:, 0, :, None] == unknowns, unknowns[None, :, None], 0), axis=1
    ).astype(jnp.int32)
    dof_inv = dof_inv[:, None, :]

    vec = (blocks, loads, width)
    vm = pltpu.VMEM
    dma = pltpu.SemaphoreType.DMA
    scratch = [
        vm((STAGES, iface, iface), F32),
        vm((slots, iface, iface), BF16),
        vm((slots, iface, iface), BF16),
        vm((NYZ, own_rows, crange), F32),
        vm((cset, crange), BF16),
        vm((cset, crange), BF16),
        vm((slots, corners, half), F32),
        vm((slots + 1, 8, width), F32),
        vm((NX * NK, 2, 8, width), F32),
        vm((slots, width, half), F32),
        vm((slots, width, half), BF16),
        vm((slots, width, half), BF16),
        vm((slots, width, half), BF16),
        vm((slots, width, half), BF16),
        vm((cset, NX * NK * 2 * width), BF16),
        vm((coarse, 2 * width), BF16),
        vm((ITERS, NK, NX, loads, 2 * width), F32),
        vm((ITERS, NY, loads, cset + width), F32),
        vm((ITERS, NZ, loads, cset + width), F32),
        vm((ITERS, NK, loads, crange), F32),
        vm((ITERS, NX, loads, crange), F32),
        vm((ITERS, NYZ, loads, crange), F32),
        vm((ITERS,) + vec, F32),
        vm((ITERS,) + vec, F32),
        vm((ITERS,) + vec, F32),
        vm((ITERS,) + vec, F32),
        vm(vec, F32),
        vm((slots, rows3, half), BF16),
        vm((slots, rows3, half), BF16),
        vm((slots, rows3, half), BF16),
        vm(vec, F32),
        vm(vec, F32),
        vm(vec, F32),
        vm(vec, F32),
        vm(vec, F32),
        vm(vec, F32),
        vm(vec, F32),
        vm(vec, F32),
        vm(vec, F32),
        vm(vec, F32),
        vm((4, loads, width), F32),
        vm((rows3, coarse), BF16),
        vm((NX, loads, width), F32),
        vm((NK, loads, width), F32),
        vm((NYZ, loads, width), F32),
        dma((slots,)),
        dma,
        dma,
        dma,
        dma,
        dma,
        dma((2, NX * NK - 1)),
        dma((2, NX * NK)),
        dma((NYZ - 1,)),
        dma((NYZ,)),
        dma((ITERS, NX - 1)),
        dma((ITERS, NX)),
        dma((ITERS, NK - 1)),
        dma((ITERS, NK)),
        dma((ITERS, NY - 1)),
        dma((ITERS, NY)),
        dma((ITERS, NZ - 1)),
        dma((ITERS, NZ)),
        dma((ITERS, NK - 1)),
        dma((ITERS, NK)),
        dma((ITERS, NX - 1)),
        dma((ITERS, NX)),
        dma((ITERS, NYZ - 1)),
        dma((ITERS, NYZ)),
        dma((ITERS,)),
        dma((ITERS,)),
        dma((ITERS,)),
        dma((ITERS,)),
        dma((NX - 1,)),
        dma((NX,)),
        dma((NK - 1,)),
        dma((NK,)),
        dma((NYZ - 1,)),
        dma((NYZ,)),
    ]
    in_vmem = pl.BlockSpec(memory_space=pltpu.VMEM)
    in_smem = pl.BlockSpec(memory_space=pltpu.SMEM)
    in_place = pl.BlockSpec(memory_space=pl.ANY)
    solved, resid = pl.pallas_call(
        kernel,
        name="feti",
        out_shape=[jax.ShapeDtypeStruct(vec, F32)] * 2,
        in_specs=[in_place, in_place] + [in_vmem] * 4 + [in_smem] * 2 + [in_vmem] * 2,
        out_specs=[in_vmem] * 2,
        scratch_shapes=scratch,
        compiler_params=pltpu.CompilerParams(
            collective_id=0, has_side_effects=True, vmem_limit_bytes=67043328
        ),
    )(flex, coarse_inverse, cpl, weight, rhs, info, own_partner, partner_inv, dof, dof_inv)

    def outer(value):
        value = value.reshape(slots, links, loads, width).transpose(0, 2, 1, 3)
        return value[None, None]

    return outer(solved), outer(resid)


def solution(mesh):
    in_specs = (
        P("row", "col", None, None, None),
        P("row", "col", None, None, None),
        P(("row", "col"), None),
        P("row", "col", None, None, None),
        P("row", "col", None, None, None, None),
        P("row", "col"),
        P("row", "col", None, None),
        P("row", "col", None, None, None),
        P("row", "col", None, None),
    )
    out_specs = (P("row", "col", None, None, None, None), P("row", "col", None, None, None, None))
    return jax.shard_map(local, mesh=mesh, in_specs=in_specs, out_specs=out_specs, check_vma=False)
```

time: 975 us -> 136 us (0.14)
  blocking collectives: 435 us -> 0 us
  waiting for transfers between devices: 396 us -> 0 us
  Pallas kernels: 0 us -> 126 us
  matrix products: 96.9 us -> 0 us
  between operations: 15 us -> 1.32 us
  starting transfers between devices: 10.6 us -> 0 us
    psum x3 -> x0, waiting for transfers between devices: 375 us -> none  [local(): total_load = lax.psum(apply_local_load, ('row', 'col'))]
    psum x5 -> x0, blocking collectives: 327 us -> none  [the longest x3 192 us: precond_norm(): return lax.psum(local_inner(resid_now, precond_now), ('row', 'col'))]
    pallas_call x0 -> x1, Pallas kernels: none -> 126 us  [local(): pl.pallas_call(kernel, name='feti', out_shape=[jax.ShapeDtypeStruct(vec,...]
    all_gather x3 -> x0, blocking collectives: 108 us -> none  [local(): corner_answer = lax.all_gather(own_rows, ('row', 'col'), axis=1, tiled=True)]
    dot_general x31 -> x0, matrix products: 96.9 us -> none  [the longest x3 61.1 us: local(): answer = jnp.einsum('sab,sqb->sqa', flex_local, force_full, precision=HIGH)]
    ppermute x8 -> x0, waiting for transfers between devices: 20.8 us -> none  [shifted(): lax.ppermute(x, axis, [(i, (i + by) % devices) for i in range(devices)])]
    ppermute x8 -> x0, starting transfers between devices: 10.5 us -> none  [shifted(): lax.ppermute(x, axis, [(i, (i + by) % devices) for i in range(devices)])]
  transfers between devices with their start and end apart: 11 -> 0, of which waited for: 9 -> 0; matrix products, arithmetic and copies ran while one was open for 6% -> 0% of each run, Pallas kernels for 0% -> 0%
where the time goes in v1:
time: 136 us; the launch traced here: 135 us
  Pallas kernels  126 us (93%)
  local copies, waits for them, and re-layouts  5.61 us (4%)
  other arithmetic  2.57 us (2%)
    pallas_call x1, Pallas kernels, local(): pl.pallas_call(kernel, name='feti', out_shape=[jax.ShapeDtypeStruct(vec,...  126 us

profile of v1, /device:TPU:1, one launch (start us, length us, event | category | flops | bytes accessed | tf_op | source)
XLA Modules:
  0.0 135.2 jit_solution(614685497633475430)
XLA Ops:
  1.3 0.8 copy.15
  2.1 0.7 select_reduce_fusion.1.partner_inv
  2.7 0.7 convert_reduce_fusion
  3.4 0.1 convert_element_type.15
  3.5 0.7 eq.31
  4.2 0.5 select_reduce_fusion
  4.8 0.6 broadcast_in_dim.52.dof_inv
  5.4 0.7 pad_maximum_fusion.info
  6.1 1.6 %copy.14 = f32[5,4,16,128]{3,2,1,0:T(8,128)} copy(f32[5,4,16,128]{3,1,2,0:T(4,128)} %bitcast.26) | data formatting | bytes 327680 | tf_op jit(solution)/shard_map/transpose | solution.py:476
  7.6 125.7 %feti.1 = (f32[20,16,128]{2,1,0:T(8,128)}, f32[20,16,128]{2,1,0:T(8,128)}) custom-call(f32[5,1024,1024]{2,1,0:T(8,128)} %bitcast.21, f32[48,6144]{1,0:T(8,128)} %cinv.1, f32[5,24,1024]{2,1,0:T(8,128)} %bitcast.23, f32[20,1,128]{2,1,0:T(1,128)} %bitcast.28, f32[20,16,128]{2,1,0:T(8,128)} %bitcast.22, f32[6,8,128]{2,1,0:T(8,128)} %pad_maximum_fusion.info, ...), custom_call_target="tpu_custom_call" | custom-call | tf_op jit(solution)/shard_map/feti/pallas_call | solution.py:582
  133.3 1.8 %copy_bitcast_fusion = (f32[1,1,5,16,4,128]{5,4,3,2,1,0:T(4,128)}, f32[1,1,5,16,4,128]{5,4,3,2,1,0:T(4,128)}) fusion(f32[5,4,16,128]{3,2,1,0:T(8,128)} %bitcast.25, f32[5,4,16,128]{3,2,1,0:T(8,128)} %bitcast.24), kind=kLoop, calls=%fused_computation.2 | loop fusion | bytes 655360 | tf_op jit(solution)/shard_map/broadcast_in_dim | solution.py:596
  (4 shorter events, 0.0 us)

commit v2 on v1

v2 whole, which is shorter than its diff:
```python
import functools

import jax
import jax.numpy as jnp
from jax import lax
from jax.experimental import pallas as pl
from jax.experimental.pallas import tpu as pltpu
from jax.sharding import PartitionSpec as P

ITERS = 3
NX, NZ, NY, NK = 4, 4, 4, 2
NYZ = NZ * NY
STAGES = 3

MESH = pl.DeviceIdType.MESH
F32 = jnp.float32
BF16 = jnp.bfloat16
NT = (((1,), (1,)), ((), ()))
NN = (((1,), (0,)), ((), ()))


def split2(value):
    high = value.astype(BF16)
    low = (value - high.astype(F32)).astype(BF16)
    return high, low


def split3(value):
    high = value.astype(BF16)
    rest = value - high.astype(F32)
    middle = rest.astype(BF16)
    low = (rest - middle.astype(F32)).astype(BF16)
    return high, middle, low


def stack3(value):
    return jnp.concatenate(split3(value), axis=0)


def dot(left, right, dims):
    return lax.dot_general(left, right, dims, preferred_element_type=F32)


def sum3(value):
    rows = value.shape[0] // 3
    return value[2 * rows :] + value[rows : 2 * rows] + value[:rows]


def rcopy(src, dst, send, recv, device):
    return pltpu.make_async_remote_copy(
        src_ref=src,
        dst_ref=dst,
        send_sem=send,
        recv_sem=recv,
        device_id=device,
        device_id_type=MESH,
    )


def group_start(src, buf, mine, send, recv, peers):
    for i, (device, _) in enumerate(peers):
        rcopy(src, buf.at[mine], send.at[i], recv.at[mine], device).start()


def group_wait(src, buf, send, recv, peers):
    for i, (device, theirs) in enumerate(peers):
        rcopy(src, buf.at[theirs], send.at[i], recv.at[theirs], device).wait_recv()
    for i, (device, theirs) in enumerate(peers):
        rcopy(src, buf.at[theirs], send.at[i], recv.at[theirs], device).wait_send()


def kernel(
    flex, cinv, cpl_in, weight_in, rhs_in, dof_in, map_in, partner, counts,
    x_out, r_out,
    stage, flex_hi, flex_lo, m32, m2, cpl, weight, rhs, dof, rowmap, dof_inv, cplp, info, infop,
    maps_yz, maps_xc, w32, wo, wp, scatter, pick, tbuf, cbuf, xbuf, y1buf, z1buf, y2buf, z2buf,
    psend, precv, qsend, qrecv, gsend, frecv, usend, urecv,
    vblk, vsp, gsp, fsp, yv, tv, dv, sv, zv, rv, mask, ulink, clink, cface, sc,
    pxbuf, pcbuf, pybuf,
    flex_sem, load_sem, mloc_sem, info_s, info_r, cpl_s, cpl_r, mapa_s, mapa_r, mapb_s, mapb_r,
    m_s, m_r, t_s, t_r, c_s, c_r, x_s, x_r, y1_s, y1_r, z1_s, z1_r, y2_s, y2_r, z2_s, z2_r,
    p_s, p_r, q_s, q_r, f_s, f_r, u_s, u_r, px_s, px_r, pc_s, pc_r, py_s, py_r,
):
    slots, iface = flex.shape[:2]
    half = iface // 2
    links, width = dof.shape[1:]
    loads = rhs.shape[1]
    corners = cpl.shape[1]
    own_rows, coarse = cinv.shape
    nxc = NX * NK
    kset = coarse // nxc
    rset = own_rows * nxc
    khalf = kset // 2
    blocks = slots * links
    tiles = 2 * width

    row, col = lax.axis_index("row"), lax.axis_index("col")
    cz = lax.div(col, NY * NK)
    cy = lax.rem(lax.div(col, NK), NY)
    ck = lax.rem(col, NK)
    cols = NZ * NY * NK
    me_yz = cz * NY + cy
    me_xc = ck * NX + row
    prev = (row, lax.rem(col + cols - 1, cols))
    nxt = (row, lax.rem(col + 1, cols))

    def device(x, z, y, k):
        return (x, (z * NY + y) * NK + k)

    def turn(value, by, size):
        return lax.rem(value + by, size)

    xs = [(device(turn(row, i, NX), cz, cy, ck), turn(row, i, NX)) for i in (2, 1, 3)]
    ys = [(device(row, cz, turn(cy, i, NY), ck), turn(cy, i, NY)) for i in (2, 1, 3)]
    zs = [(device(row, turn(cz, i, NZ), cy, ck), turn(cz, i, NZ)) for i in (2, 1, 3)]
    cs = [(device(row, cz, cy, 1 - ck), 1 - ck)]
    order = sorted(
        [(i, j) for i in range(NZ) for j in range(NY) if (i, j) != (0, 0)],
        key=lambda ij: -(min(ij[0], NZ - ij[0]) + min(ij[1], NY - ij[1])),
    )
    yzs = [
        (device(row, turn(cz, i, NZ), turn(cy, j, NY), ck), turn(cz, i, NZ) * NY + turn(cy, j, NY))
        for i, j in order
    ]
    xcs = [
        (device(turn(row, i, NX), cz, cy, turn(ck, j, NK)), turn(ck, j, NK) * NX + turn(row, i, NX))
        for i in (2, 1, 3, 0)
        for j in range(NK)
        if (i, j) != (0, 0)
    ]

    barrier = pltpu.get_barrier_semaphore()
    everyone = [d for d, _ in yzs] + [d for d, _ in xcs] + [prev, nxt]
    for d in everyone:
        pl.semaphore_signal(barrier, inc=1, device_id=d, device_id_type=MESH)

    def flex_copy(s):
        return pltpu.make_async_copy(flex.at[s], stage.at[s % STAGES], flex_sem.at[s])

    def m_part(other):
        return cinv.at[:, pl.ds(pl.multiple_of(other * kset, 128), kset)]

    loaded = [
        pltpu.make_async_copy(src, dst, load_sem.at[i])
        for i, (src, dst) in enumerate(
            [(map_in, rowmap), (dof_in, dof), (rhs_in, rhs), (weight_in, weight), (cpl_in, cpl)]
        )
    ]
    for copy in loaded:
        copy.start()
    m_local = pltpu.make_async_copy(m_part(me_xc), m32.at[me_xc], mloc_sem)
    m_local.start()
    for s in range(STAGES):
        flex_copy(s).start()

    for s in range(slots):
        live = jnp.where(s < counts[0, 0], 1.0, 0.0).astype(F32)
        info[s] = jnp.broadcast_to(live, (8, width))
    loaded[0].wait()
    lane8 = lax.broadcasted_iota(jnp.int32, (8, width), 1)
    found = jnp.full((8, width), -1, jnp.int32)
    for s in range(slots):
        ids = jnp.broadcast_to(rowmap[s : s + 1, :], (8, corners))
        ids = jnp.concatenate([ids, jnp.zeros((8, width - corners), jnp.int32)], axis=1)
        if s:
            ids = pltpu.roll(ids, s * corners, 1)
        inside = jnp.logical_and(lane8 >= s * corners, lane8 < (s + 1) * corners)
        found = jnp.where(inside, ids, found)
    info[slots] = found.astype(F32)

    pl.semaphore_wait(barrier, len(everyone))

    info_copy = rcopy(info, infop, info_s, info_r, nxt)
    info_copy.start()
    loaded[4].wait()
    cpl_copy = rcopy(cpl.at[:, :, half:], cplp, cpl_s, cpl_r, nxt)
    cpl_copy.start()
    for i, (d, other) in enumerate(xcs):
        rcopy(m_part(other), m32.at[me_xc], m_s.at[i], m_r.at[me_xc], d).start()
    map_groups = [(maps_yz, me_yz, mapa_s, mapa_r, yzs), (maps_xc, me_xc, mapb_s, mapb_r, xcs)]

    def send_maps(src, h):
        for buf, mine, send, recv, peers in map_groups:
            for i, (d, _) in enumerate(peers):
                rcopy(src, buf.at[mine, h], send.at[h, i], recv.at[h, mine], d).start()
            buf[mine, h] = src[...]

    def wait_maps(h, group):
        buf, _, send, recv, peers = map_groups[group]
        src = (info, infop)[h].at[slots]
        for i, (d, other) in enumerate(peers):
            cp = rcopy(src, buf.at[other, h], send.at[h, i], recv.at[h, other], d)
            cp.wait_recv()
            cp.wait_send()

    send_maps(info.at[slots], 0)

    w32[...] = jnp.zeros_like(w32)

    def build_coupling(source, out):
        for s in range(slots):
            w32[s, s * corners : (s + 1) * corners, :] = source[s, :, 0:half]
        for s in range(slots):
            high, low = split2(w32[s])
            out[s, 0:width] = high
            out[s, width:tiles] = low

    build_coupling(cpl, wo)
    tv[...] = jnp.zeros_like(tv)
    dv[...] = jnp.zeros_like(dv)
    sv[...] = jnp.zeros_like(sv)
    x_out[...] = jnp.zeros_like(x_out)
    sc[0] = jnp.ones_like(sc[0])
    sc[1] = jnp.zeros_like(sc[1])
    sc[2] = jnp.zeros_like(sc[2])
    sc[3] = jnp.zeros_like(sc[3])

    loaded[1].wait()
    sub = lax.broadcasted_iota(jnp.int32, (width, width), 0)
    numbers = lane8.astype(F32).astype(BF16)
    for b in range(blocks):
        ids = dof[b // links, b % links : b % links + 1, :]
        hit = jnp.where(sub == ids, 1.0, 0.0).astype(BF16)
        dof_inv[b] = dot(numbers, hit, NT).astype(jnp.int32)

    inverse = {}
    for k in range(links):
        for p in range(slots):
            at = jnp.int32(0)
            for j in range(1, slots):
                at = jnp.where(partner[k, j] == p, j, at)
            inverse[k, p] = at

    loaded[2].wait()
    loaded[3].wait()
    info_copy.wait_recv()
    send_maps(infop.at[slots], 1)

    def weight_of(b):
        return weight[b // links, b % links : b % links + 1, :]

    for b in range(blocks):
        s, k = b // links, b % links
        live = info[s] * infop[partner[k, s]]
        live = jnp.concatenate([live] * (loads // 8), axis=0)
        mask[b] = live
        resid = live * rhs[s, :, k, :]
        rv[b] = resid
        yv[b] = resid
        zv[b] = weight_of(b) * resid

    cpl_copy.wait_recv()
    build_coupling(cplp, wp)

    lane = lax.broadcasted_iota(jnp.int32, (loads, width), 1)
    load_id = lax.broadcasted_iota(jnp.int32, (loads, width), 0)

    def total(first, second):
        return jnp.sum(jnp.sum(first * second, axis=0), axis=1, keepdims=True)

    def scalar_terms(packed):
        z, y = zv[...], yv[...]
        found = [total(rv[...], z), total(z, y), total(z, sv[...]), total(dv[...], y)]
        tile = jnp.zeros((loads, width), F32)
        for i, value in enumerate(found):
            at = lane == (4 * load_id + i if packed else i)
            tile = jnp.where(at, value, tile)
        return tile

    def update(tile, packed, first):
        rz, zy, zs_, dy = [
            jnp.broadcast_to(
                jnp.sum(
                    jnp.where(lane == (4 * load_id + i if packed else i), tile, 0.0),
                    axis=1,
                    keepdims=True,
                ),
                tile.shape,
            )
            for i in range(4)
        ]
        beta = rz / sc[0]
        if first is not None:
            beta = jnp.where(first, 0.0, beta)
        curv = zy + beta * (zs_ + dy) + beta * beta * sc[1]
        alpha = rz / curv
        sc[0], sc[1], sc[2], sc[3] = rz, curv, alpha, beta
        direction = zv[...] + beta[None] * dv[...]
        image = yv[...] + beta[None] * sv[...]
        dv[...] = direction
        sv[...] = image
        x_out[...] = x_out[...] + alpha[None] * direction
        resid = rv[...] - alpha[None] * image
        rv[...] = resid
        return resid

    def put3(ref, s, k, value):
        for i, part in enumerate(split3(value)):
            ref[s, i * loads : (i + 1) * loads, k * width : (k + 1) * width] = part

    def take(value, index):
        return jnp.take_along_axis(value, index, axis=1, mode="promise_in_bounds")

    def convert(s):
        flex_copy(s).wait()
        here = s % STAGES

        def chunk(i, _):
            at = pl.ds(pl.multiple_of(i * 64, 64), 64)
            high, low = split2(stage[here, at, :])
            flex_hi[s, at, :] = high
            flex_lo[s, at, :] = low
            return 0

        lax.fori_loop(0, iface // 64, chunk, 0)
        if s + STAGES < slots:
            flex_copy(s + STAGES).start()

    def local_answers(it, first, last):
        def one(s, _):
            left = jnp.concatenate([vsp[s], fsp[s]], axis=1)
            for n in range(iface // 256):
                at = slice(n * 256, (n + 1) * 256)
                out = dot(left, flex_hi[s, :, at], NN) + dot(left, flex_lo[s, :, at], NN)
                out = sum3(out)
                for h in range(2):
                    piece = out[:, h * width : (h + 1) * width]
                    k = 2 * n + h
                    if k < links:
                        ulink[s * links + k] = piece
                    else:
                        usend[it, s * links + k - links] = piece
            return 0

        lax.fori_loop(first, last, one, 0)

    def both(value):
        return value[:, :width] + value[:, width:]

    def body(it, _):
        for b in range(blocks):
            value = weight_of(b) * yv[b]
            vblk[b] = value
            put3(vsp, b // links, b % links, value)
        for b in range(blocks):
            p, k = b // links, b % links
            from_block = inverse[k, p] * links + k
            index = jnp.concatenate([dof_inv[from_block]] * (loads // 8), axis=0)
            value = -take(vblk[from_block], index)
            gsend[it, b] = value
            put3(gsp, p, k, value)

        def terms(blocks3, factors):
            found = None
            for s in range(slots):
                part = dot(blocks3[s], factors[s], NT)
                found = part if found is None else found + part
            return both(sum3(found))

        tbuf[it, me_yz, :, 0:width] = terms(vsp, wo)
        tbuf[it, me_yz, :, width:tiles] = terms(gsp, wp)
        group_start(tbuf.at[it, me_yz], tbuf.at[it], me_yz, t_s.at[it], t_r.at[it], yzs)
        force_copy = rcopy(gsend.at[it], frecv.at[it], f_s.at[it], f_r.at[it], prev)
        force_copy.start()
        tile = scalar_terms(False)

        @pl.when(it == 0)
        def _():
            wait_maps(0, 0)
            wait_maps(1, 0)

            def rows(p, _):
                base = (lax.rem(p, NX) * cols + me_yz * NK + lax.div(p, NX)) * own_rows
                index = lax.broadcasted_iota(jnp.int32, (own_rows, width), 0) + base
                index = index.astype(F32)
                at = pl.ds(pl.multiple_of(p * own_rows, own_rows), own_rows)
                for q in range(NYZ):
                    for h in range(2):
                        hit = jnp.where(index == maps_yz[q, h, 0:1, :], 1.0, 0.0)
                        lo = (2 * q + h) * width
                        scatter[at, lo : lo + width] = hit.astype(BF16)
                return 0

            lax.fori_loop(0, nxc, rows, 0)
            for s in range(STAGES):
                convert(s)

        group_wait(tbuf.at[it, me_yz], tbuf.at[it], t_s.at[it], t_r.at[it], yzs)
        gathered = jnp.concatenate([stack3(tbuf[it, q]) for q in range(NYZ)], axis=1)
        cbuf[it, ck, :, 0:rset] = sum3(dot(gathered, scatter[...], NT))
        cbuf[it, ck, :, rset : rset + width] = tile
        group_start(cbuf.at[it, ck], cbuf.at[it], ck, c_s.at[it], c_r.at[it], cs)
        group_wait(cbuf.at[it, ck], cbuf.at[it], c_s.at[it], c_r.at[it], cs)
        xbuf[it, row] = cbuf[it, 0] + cbuf[it, 1]
        group_start(xbuf.at[it, row], xbuf.at[it], row, x_s.at[it], x_r.at[it], xs)

        force_copy.wait_recv()
        for b in range(blocks):
            put3(fsp, b // links, b % links, frecv[it, b])
        local_answers(it, 0, 3)

        @pl.when(it == 0)
        def _():
            m_local.wait()
            for i, (d, other) in enumerate(xcs):
                cp = rcopy(m_part(other), m32.at[other], m_s.at[i], m_r.at[other], d)
                cp.wait_recv()
                cp.wait_send()
            for b in range(nxc):
                high, low = split2(m32[b])
                m2[b * own_rows : (b + 1) * own_rows, :] = high
                m2[rset + b * own_rows : rset + (b + 1) * own_rows, :] = low

        group_wait(xbuf.at[it, row], xbuf.at[it], x_s.at[it], x_r.at[it], xs)
        load = xbuf[it, 0] + xbuf[it, 1] + xbuf[it, 2] + xbuf[it, 3]
        left = stack3(load[:, :rset])
        answer = sum3(dot(jnp.concatenate([left, left], axis=1), m2[...], NN))
        y1buf[it, cy, :, 0:khalf] = answer[:, :khalf]
        y1buf[it, cy, :, khalf : khalf + width] = load[:, rset:]
        z1buf[it, cz] = answer[:, khalf:]
        group_start(y1buf.at[it, cy], y1buf.at[it], cy, y1_s.at[it], y1_r.at[it], ys)
        group_start(z1buf.at[it, cz], z1buf.at[it], cz, z1_s.at[it], z1_r.at[it], zs)

        @pl.when(it == 0)
        def _():
            for s in range(STAGES, slots):
                convert(s)

        local_answers(it, 3, slots)

        group_wait(y1buf.at[it, cy], y1buf.at[it], y1_s.at[it], y1_r.at[it], ys)
        group_wait(z1buf.at[it, cz], z1buf.at[it], z1_s.at[it], z1_r.at[it], zs)
        z2buf[it, cz] = y1buf[it, 0] + y1buf[it, 1] + y1buf[it, 2] + y1buf[it, 3]
        y2buf[it, cy] = z1buf[it, 0] + z1buf[it, 1] + z1buf[it, 2] + z1buf[it, 3]
        group_start(z2buf.at[it, cz], z2buf.at[it], cz, z2_s.at[it], z2_r.at[it], zs)
        group_start(y2buf.at[it, cy], y2buf.at[it], cy, y2_s.at[it], y2_r.at[it], ys)
        answer_copy = rcopy(usend.at[it], urecv.at[it], u_s.at[it], u_r.at[it], nxt)
        answer_copy.start()

        @pl.when(it == 0)
        def _():
            wait_maps(0, 1)
            wait_maps(1, 1)
            step = own_rows

            def rows(b, _):
                index = lax.broadcasted_iota(jnp.int32, (step, width), 0) + (me_xc * kset + b * step)
                index = index.astype(F32)
                at = pl.ds(pl.multiple_of(b * step, step), step)
                for q in range(nxc):
                    for h in range(2):
                        hit = jnp.where(index == maps_xc[q, h, 0:1, :], 1.0, 0.0)
                        lo = (2 * q + h) * width
                        pick[at, lo : lo + width] = hit.astype(BF16)
                return 0

            lax.fori_loop(0, kset // step, rows, 0)

        group_wait(z2buf.at[it, cz], z2buf.at[it], z2_s.at[it], z2_r.at[it], zs)
        group_wait(y2buf.at[it, cy], y2buf.at[it], y2_s.at[it], y2_r.at[it], ys)
        first = z2buf[it, 0] + z2buf[it, 1] + z2buf[it, 2] + z2buf[it, 3]
        second = y2buf[it, 0] + y2buf[it, 1] + y2buf[it, 2] + y2buf[it, 3]
        scalars = first[:, khalf:]
        left = stack3(jnp.concatenate([first[:, :khalf], second], axis=1))
        found = sum3(dot(left, pick[...], NN))
        for q in range(nxc):
            psend[it, q // NX, q % NX] = found[:, q * tiles : (q + 1) * tiles]
        core_copy = rcopy(
            psend.at[it, 1 - ck], precv.at[it], p_s.at[it], p_r.at[it], cs[0][0]
        )
        core_copy.start()
        core_copy.wait()
        for q in range(NX):
            qsend[it, q] = psend[it, ck, q] + precv[it, q]
        for i, (d, other) in enumerate(xs):
            rcopy(
                qsend.at[it, other], qrecv.at[it, row], q_s.at[it, i], q_r.at[it, row], d
            ).start()
        qrecv[it, row] = qsend[it, row]

        @pl.when(it > 0)
        def _():
            resid = update(scalars, False, it == 1)
            for b in range(blocks):
                zv[b] = weight_of(b) * resid[b]

        for i, (d, other) in enumerate(xs):
            cp = rcopy(
                qsend.at[it, other], qrecv.at[it, other], q_s.at[it, i], q_r.at[it, other], d
            )
            cp.wait_recv()
            cp.wait_send()
        picked = stack3(qrecv[it, 0] + qrecv[it, 1] + qrecv[it, 2] + qrecv[it, 3])
        to_link = jnp.concatenate([picked[:, :width]] * 2, axis=1)
        to_face = jnp.concatenate([picked[:, width:]] * 2, axis=1)
        for s in range(slots):
            found = sum3(dot(to_link, wo[s], NN))
            other = sum3(dot(to_face, wp[s], NN))
            for k in range(links):
                clink[s * links + k] = found[:, k * width : (k + 1) * width]
                cface[s * links + k] = other[:, k * width : (k + 1) * width]

        answer_copy.wait_recv()
        answer_copy.wait_send()
        force_copy.wait_send()
        alpha, beta = sc[2], sc[3]
        for b in range(blocks):
            s, k = b // links, b % links
            facing = partner[k, s] * links + k
            index = jnp.broadcast_to(dof[s, k : k + 1, :], (loads, width))
            far = take(urecv[it, facing] + cface[facing], index)
            image = (ulink[b] + clink[b] - far) * mask[b]
            image = image + beta * tv[b]
            tv[b] = jnp.where(it == 0, 0.0, image)
            yv[b] = jnp.where(it == 0, image, yv[b] - alpha * image)
        return 0

    lax.fori_loop(0, ITERS, body, 0)

    info_copy.wait_send()
    cpl_copy.wait_send()
    pxbuf[row] = jnp.sum(scalar_terms(True), axis=0, keepdims=True)
    group_start(pxbuf.at[row], pxbuf, row, px_s, px_r, xs)
    group_wait(pxbuf.at[row], pxbuf, px_s, px_r, xs)
    pcbuf[ck] = pxbuf[0] + pxbuf[1] + pxbuf[2] + pxbuf[3]
    group_start(pcbuf.at[ck], pcbuf, ck, pc_s, pc_r, cs)
    group_wait(pcbuf.at[ck], pcbuf, pc_s, pc_r, cs)
    pybuf[me_yz] = pcbuf[0] + pcbuf[1]
    group_start(pybuf.at[me_yz], pybuf, me_yz, py_s, py_r, yzs)
    group_wait(pybuf.at[me_yz], pybuf, py_s, py_r, yzs)
    line = pybuf[0]
    for b in range(1, NYZ):
        line = line + pybuf[b]
    r_out[...] = update(jnp.broadcast_to(line, (loads, width)), True, None)


def local(
    flexibility,
    coupling,
    coarse_inverse,
    precon_weight,
    right_side,
    counts,
    partner,
    dof_index,
    corner_map,
):
    flex = flexibility[0, 0]
    cpl = coupling[0, 0]
    slots, iface = flex.shape[:2]
    half = iface // 2
    links, width = dof_index.shape[3:]
    loads = right_side.shape[3]
    own_rows, coarse = coarse_inverse.shape
    corners = corner_map.shape[-1]
    blocks = slots * links
    nxc = NX * NK
    kset, rset = coarse // nxc, own_rows * nxc
    rows3 = 3 * loads
    pair = 2 * width

    vec = (blocks, loads, width)
    per = (ITERS,)
    vm = pltpu.VMEM
    dma = pltpu.SemaphoreType.DMA
    scratch = [
        vm((STAGES, iface, iface), F32),
        vm((slots, iface, iface), BF16),
        vm((slots, iface, iface), BF16),
        vm((nxc, own_rows, kset), F32),
        vm((2 * rset, kset), BF16),
        vm(cpl.shape, F32),
        vm((slots, links, width), F32),
        vm((slots, loads, links, width), F32),
        vm((slots, links, width), jnp.int32),
        vm((slots, corners), jnp.int32),
        vm((blocks, 8, width), jnp.int32),
        vm((slots, corners, half), F32),
        vm((slots + 1, 8, width), F32),
        vm((slots + 1, 8, width), F32),
        vm((NYZ, 2, 8, width), F32),
        vm((nxc, 2, 8, width), F32),
        vm((slots, width, half), F32),
        vm((slots, pair, half), BF16),
        vm((slots, pair, half), BF16),
        vm((rset, NYZ * pair), BF16),
        vm((kset, nxc * pair), BF16),
        vm(per + (NYZ, loads, pair), F32),
        vm(per + (NK, loads, rset + width), F32),
        vm(per + (NX, loads, rset + width), F32),
        vm(per + (NY, loads, kset // 2 + width), F32),
        vm(per + (NZ, loads, kset // 2), F32),
        vm(per + (NY, loads, kset // 2), F32),
        vm(per + (NZ, loads, kset // 2 + width), F32),
        vm(per + (NK, NX, loads, pair), F32),
        vm(per + (NX, loads, pair), F32),
        vm(per + (NX, loads, pair), F32),
        vm(per + (NX, loads, pair), F32),
        vm(per + vec, F32),
        vm(per + vec, F32),
        vm(per + vec, F32),
        vm(per + vec, F32),
        vm(vec, F32),
        vm((slots, rows3, half), BF16),
        vm((slots, rows3, half), BF16),
        vm((slots, rows3, half), BF16),
    ]
    scratch += [vm(vec, F32)] * 10
    scratch += [
        vm((4, loads, width), F32),
        vm((NX, 1, width), F32),
        vm((NK, 1, width), F32),
        vm((NYZ, 1, width), F32),
        dma((slots,)),
        dma((5,)),
        dma,
        dma,
        dma,
        dma,
        dma,
        dma((2, NYZ - 1)),
        dma((2, NYZ)),
        dma((2, nxc - 1)),
        dma((2, nxc)),
        dma((nxc - 1,)),
        dma((nxc,)),
    ]
    for size in (NYZ, NK, NX, NY, NZ, NY, NZ):
        scratch += [dma(per + (size - 1,)), dma(per + (size,))]
    scratch += [dma(per)] * 2 + [dma(per + (NX - 1,)), dma(per + (NX,))] + [dma(per)] * 4
    for size in (NX, NK, NYZ):
        scratch += [dma((size - 1,)), dma((size,))]
    in_vmem = pl.BlockSpec(memory_space=pltpu.VMEM)
    in_smem = pl.BlockSpec(memory_space=pltpu.SMEM)
    in_place = pl.BlockSpec(memory_space=pl.ANY)
    solved, resid = pl.pallas_call(
        kernel,
        name="feti",
        out_shape=[jax.ShapeDtypeStruct(vec, F32)] * 2,
        in_specs=[in_place] * 7 + [in_smem] * 2,
        out_specs=[in_vmem] * 2,
        scratch_shapes=scratch,
        compiler_params=pltpu.CompilerParams(
            collective_id=0, has_side_effects=True, vmem_limit_bytes=67043328
        ),
    )(
        flex,
        coarse_inverse,
        cpl,
        precon_weight[0, 0],
        right_side[0, 0],
        dof_index[0, 0],
        corner_map[0, 0],
        partner[0, 0],
        counts,
    )

    def outer(value):
        value = value.reshape(slots, links, loads, width).transpose(0, 2, 1, 3)
        return value[None, None]

    return outer(solved), outer(resid)


def solution(mesh):
    in_specs = (
        P("row", "col", None, None, None),
        P("row", "col", None, None, None),
        P(("row", "col"), None),
        P("row", "col", None, None, None),
        P("row", "col", None, None, None, None),
        P("row", "col"),
        P("row", "col", None, None),
        P("row", "col", None, None, None),
        P("row", "col", None, None),
    )
    out_specs = (P("row", "col", None, None, None, None), P("row", "col", None, None, None, None))
    return jax.shard_map(local, mesh=mesh, in_specs=in_specs, out_specs=out_specs, check_vma=False)
```

time: 136 us -> 117 us (0.86)
  Pallas kernels: 126 us -> 112 us
  other arithmetic: 2.57 us -> 0 us
  local copies, waits for them, and re-layouts: 5.61 us -> 3.12 us
    pallas_call x1, Pallas kernels: 126 us -> 112 us  [local(): pl.pallas_call(kernel, name='feti', out_shape=[jax.ShapeDtypeStruct(vec,...]
    transpose x1 -> x0, local copies, waits for them, and re-layouts: 1.59 us -> none  [local(): rhs = right_side[0, 0].transpose(0, 2, 1, 3).reshape(blocks, loads, width)]
where the time goes in v2:
time: 117 us; the launch traced here: 116 us
  Pallas kernels  112 us (96%)
  local copies, waits for them, and re-layouts  3.12 us (3%)
  between operations  1.28 us (1%)
    pallas_call x1, Pallas kernels, local(): pl.pallas_call(kernel, name='feti', out_shape=[jax.ShapeDtypeStruct(vec,...  112 us

profile of v2, /device:TPU:1, one launch (start us, length us, event | category | flops | bytes accessed | tf_op | source)
XLA Modules:
  0.0 116.3 jit_solution(15630529697082127698)
XLA Ops:
  1.3 1.3 %copy.17 = s32[1,1,5,24]{3,2,1,0:T(8,128)} copy(s32[1,1,5,24]{3,1,2,0:T(1,128)} %param.17) | data formatting | bytes 960
  2.6 111.9 %feti.1 = (f32[20,16,128]{2,1,0:T(8,128)}, f32[20,16,128]{2,1,0:T(8,128)}) custom-call(f32[5,1024,1024]{2,1,0:T(8,128)} %bitcast.19, f32[48,6144]{1,0:T(8,128)} %cinv.1, f32[5,24,1024]{2,1,0:T(8,128)} %bitcast.20, f32[5,4,128]{2,1,0:T(4,128)} %bitcast.25, f32[5,16,4,128]{3,2,1,0:T(4,128)} %bitcast.21, s32[5,4,128]{2,1,0:T(4,128)} %bitcast.26, ...), custom_call_target="tpu_custom_call" | custom-call | tf_op jit(solution)/shard_map/feti/pallas_call | solution.py:636
  114.5 1.8 %copy_bitcast_fusion = (f32[1,1,5,16,4,128]{5,4,3,2,1,0:T(4,128)}, f32[1,1,5,16,4,128]{5,4,3,2,1,0:T(4,128)}) fusion(f32[5,4,16,128]{3,2,1,0:T(8,128)} %bitcast.23, f32[5,4,16,128]{3,2,1,0:T(8,128)} %bitcast.22), kind=kLoop, calls=%fused_computation | loop fusion | bytes 655360 | tf_op jit(solution)/shard_map/broadcast_in_dim | solution.py:660

commit v3 on v2

--- a/solution.py
+++ b/solution.py
@@ -155,18 +155,18 @@
 
     for s in range(slots):
         live = jnp.where(s < counts[0, 0], 1.0, 0.0).astype(F32)
-        info[s] = jnp.broadcast_to(live, (8, width))
+        info[s] = jnp.broadcast_to(live, (1, width))
     loaded[0].wait()
     lane8 = lax.broadcasted_iota(jnp.int32, (8, width), 1)
     found = jnp.full((8, width), -1, jnp.int32)
     for s in range(slots):
-        ids = jnp.broadcast_to(rowmap[s : s + 1, :], (8, corners))
+        ids = jnp.broadcast_to(rowmap[s], (8, corners))
         ids = jnp.concatenate([ids, jnp.zeros((8, width - corners), jnp.int32)], axis=1)
         if s:
             ids = pltpu.roll(ids, s * corners, 1)
         inside = jnp.logical_and(lane8 >= s * corners, lane8 < (s + 1) * corners)
         found = jnp.where(inside, ids, found)
-    info[slots] = found.astype(F32)
+    info[slots] = found[0:1].astype(F32)
 
     pl.semaphore_wait(barrier, len(everyone))
 
@@ -242,15 +242,12 @@
     for b in range(blocks):
         s, k = b // links, b % links
         live = info[s] * infop[partner[k, s]]
-        live = jnp.concatenate([live] * (loads // 8), axis=0)
+        live = jnp.broadcast_to(live, (loads, width))
         mask[b] = live
         resid = live * rhs[s, :, k, :]
         rv[b] = resid
         yv[b] = resid
         zv[b] = weight_of(b) * resid
-
-    cpl_copy.wait_recv()
-    build_coupling(cplp, wp)
 
     lane = lax.broadcasted_iota(jnp.int32, (loads, width), 1)
     load_id = lax.broadcasted_iota(jnp.int32, (loads, width), 0)
@@ -358,10 +355,14 @@
             return both(sum3(found))
 
         tbuf[it, me_yz, :, 0:width] = terms(vsp, wo)
+
+        @pl.when(it == 0)
+        def _():
+            cpl_copy.wait_recv()
+            build_coupling(cplp, wp)
+
         tbuf[it, me_yz, :, width:tiles] = terms(gsp, wp)
         group_start(tbuf.at[it, me_yz], tbuf.at[it], me_yz, t_s.at[it], t_r.at[it], yzs)
-        force_copy = rcopy(gsend.at[it], frecv.at[it], f_s.at[it], f_r.at[it], prev)
-        force_copy.start()
         tile = scalar_terms(False)
 
         @pl.when(it == 0)
@@ -376,31 +377,40 @@
                 at = pl.ds(pl.multiple_of(p * own_rows, own_rows), own_rows)
                 for q in range(NYZ):
                     for h in range(2):
-                        hit = jnp.where(index == maps_yz[q, h, 0:1, :], 1.0, 0.0)
-                        lo = (2 * q + h) * width
-                        scatter[at, lo : lo + width] = hit.astype(BF16)
+                        hit = jnp.where(index == maps_yz[q, h], 1.0, 0.0)
+                        scatter[q, at, h * width : (h + 1) * width] = hit.astype(BF16)
                 return 0
 
             lax.fori_loop(0, nxc, rows, 0)
             for s in range(STAGES):
                 convert(s)
 
-        group_wait(tbuf.at[it, me_yz], tbuf.at[it], t_s.at[it], t_r.at[it], yzs)
-        gathered = jnp.concatenate([stack3(tbuf[it, q]) for q in range(NYZ)], axis=1)
-        cbuf[it, ck, :, 0:rset] = sum3(dot(gathered, scatter[...], NT))
+        def spread(q):
+            return dot(stack3(tbuf[it, q]), scatter[q], NT)
+
+        found = spread(me_yz)
+        arrivals = [
+            rcopy(tbuf.at[it, me_yz], tbuf.at[it, q], t_s.at[it, i], t_r.at[it, q], d)
+            for i, (d, q) in enumerate(yzs)
+        ]
+        for copy, (_, q) in reversed(list(zip(arrivals, yzs))):
+            copy.wait_recv()
+            found = found + spread(q)
+        for copy in arrivals:
+            copy.wait_send()
+        cbuf[it, ck, :, 0:rset] = sum3(found)
         cbuf[it, ck, :, rset : rset + width] = tile
         group_start(cbuf.at[it, ck], cbuf.at[it], ck, c_s.at[it], c_r.at[it], cs)
+        force_copy = rcopy(gsend.at[it], frecv.at[it], f_s.at[it], f_r.at[it], prev)
+        force_copy.start()
         group_wait(cbuf.at[it, ck], cbuf.at[it], c_s.at[it], c_r.at[it], cs)
         xbuf[it, row] = cbuf[it, 0] + cbuf[it, 1]
         group_start(xbuf.at[it, row], xbuf.at[it], row, x_s.at[it], x_r.at[it], xs)
 
-        force_copy.wait_recv()
-        for b in range(blocks):
-            put3(fsp, b // links, b % links, frecv[it, b])
-        local_answers(it, 0, 3)
-
         @pl.when(it == 0)
         def _():
+            for s in range(STAGES, slots):
+                convert(s)
             m_local.wait()
             for i, (d, other) in enumerate(xcs):
                 cp = rcopy(m_part(other), m32.at[other], m_s.at[i], m_r.at[other], d)
@@ -421,12 +431,10 @@
         group_start(y1buf.at[it, cy], y1buf.at[it], cy, y1_s.at[it], y1_r.at[it], ys)
         group_start(z1buf.at[it, cz], z1buf.at[it], cz, z1_s.at[it], z1_r.at[it], zs)
 
-        @pl.when(it == 0)
-        def _():
-            for s in range(STAGES, slots):
-                convert(s)
-
-        local_answers(it, 3, slots)
+        force_copy.wait_recv()
+        for b in range(blocks):
+            put3(fsp, b // links, b % links, frecv[it, b])
+        local_answers(it, 0, 3)
 
         group_wait(y1buf.at[it, cy], y1buf.at[it], y1_s.at[it], y1_r.at[it], ys)
         group_wait(z1buf.at[it, cz], z1buf.at[it], z1_s.at[it], z1_r.at[it], zs)
@@ -434,8 +442,7 @@
         y2buf[it, cy] = z1buf[it, 0] + z1buf[it, 1] + z1buf[it, 2] + z1buf[it, 3]
         group_start(z2buf.at[it, cz], z2buf.at[it], cz, z2_s.at[it], z2_r.at[it], zs)
         group_start(y2buf.at[it, cy], y2buf.at[it], cy, y2_s.at[it], y2_r.at[it], ys)
-        answer_copy = rcopy(usend.at[it], urecv.at[it], u_s.at[it], u_r.at[it], nxt)
-        answer_copy.start()
+        local_answers(it, 3, slots)
 
         @pl.when(it == 0)
         def _():
@@ -449,29 +456,30 @@
                 at = pl.ds(pl.multiple_of(b * step, step), step)
                 for q in range(nxc):
                     for h in range(2):
-                        hit = jnp.where(index == maps_xc[q, h, 0:1, :], 1.0, 0.0)
-                        lo = (2 * q + h) * width
-                        pick[at, lo : lo + width] = hit.astype(BF16)
+                        hit = jnp.where(index == maps_xc[q, h], 1.0, 0.0)
+                        lo = (2 * (q % NX) + h) * width
+                        pick[q // NX, at, lo : lo + width] = hit.astype(BF16)
                 return 0
 
             lax.fori_loop(0, kset // step, rows, 0)
 
         group_wait(z2buf.at[it, cz], z2buf.at[it], z2_s.at[it], z2_r.at[it], zs)
         group_wait(y2buf.at[it, cy], y2buf.at[it], y2_s.at[it], y2_r.at[it], ys)
+        answer_copy = rcopy(usend.at[it], urecv.at[it], u_s.at[it], u_r.at[it], nxt)
+        answer_copy.start()
         first = z2buf[it, 0] + z2buf[it, 1] + z2buf[it, 2] + z2buf[it, 3]
         second = y2buf[it, 0] + y2buf[it, 1] + y2buf[it, 2] + y2buf[it, 3]
         scalars = first[:, khalf:]
         left = stack3(jnp.concatenate([first[:, :khalf], second], axis=1))
-        found = sum3(dot(left, pick[...], NN))
-        for q in range(nxc):
-            psend[it, q // NX, q % NX] = found[:, q * tiles : (q + 1) * tiles]
-        core_copy = rcopy(
-            psend.at[it, 1 - ck], precv.at[it], p_s.at[it], p_r.at[it], cs[0][0]
-        )
+        found = sum3(dot(left, pick[1 - ck], NN))
+        for q in range(NX):
+            psend[it, q] = found[:, q * tiles : (q + 1) * tiles]
+        core_copy = rcopy(psend.at[it], precv.at[it], p_s.at[it], p_r.at[it], cs[0][0])
         core_copy.start()
+        found = sum3(dot(left, pick[ck], NN))
         core_copy.wait()
         for q in range(NX):
-            qsend[it, q] = psend[it, ck, q] + precv[it, q]
+            qsend[it, q] = found[:, q * tiles : (q + 1) * tiles] + precv[it, q]
         for i, (d, other) in enumerate(xs):
             rcopy(
                 qsend.at[it, other], qrecv.at[it, row], q_s.at[it, i], q_r.at[it, row], d
@@ -573,18 +581,18 @@
         vm((slots, links, width), F32),
         vm((slots, loads, links, width), F32),
         vm((slots, links, width), jnp.int32),
-        vm((slots, corners), jnp.int32),
+        vm((slots, 1, corners), jnp.int32),
         vm((blocks, 8, width), jnp.int32),
         vm((slots, corners, half), F32),
-        vm((slots + 1, 8, width), F32),
-        vm((slots + 1, 8, width), F32),
-        vm((NYZ, 2, 8, width), F32),
-        vm((nxc, 2, 8, width), F32),
+        vm((slots + 1, 1, width), F32),
+        vm((slots + 1, 1, width), F32),
+        vm((NYZ, 2, 1, width), F32),
+        vm((nxc, 2, 1, width), F32),
         vm((slots, width, half), F32),
         vm((slots, pair, half), BF16),
         vm((slots, pair, half), BF16),
-        vm((rset, NYZ * pair), BF16),
-        vm((kset, nxc * pair), BF16),
+        vm((NYZ, rset, pair), BF16),
+        vm((NK, kset, NX * pair), BF16),
         vm(per + (NYZ, loads, pair), F32),
         vm(per + (NK, loads, rset + width), F32),
         vm(per + (NX, loads, rset + width), F32),
@@ -592,7 +600,7 @@
         vm(per + (NZ, loads, kset // 2), F32),
         vm(per + (NY, loads, kset // 2), F32),
         vm(per + (NZ, loads, kset // 2 + width), F32),
-        vm(per + (NK, NX, loads, pair), F32),
+        vm(per + (NX, loads, pair), F32),
         vm(per + (NX, loads, pair), F32),
         vm(per + (NX, loads, pair), F32),
         vm(per + (NX, loads, pair), F32),
@@ -650,7 +658,7 @@
         precon_weight[0, 0],
         right_side[0, 0],
         dof_index[0, 0],
-        corner_map[0, 0],
+        corner_map.reshape(slots, 1, corners),
         partner[0, 0],
         counts,
     )

time: 117 us -> 112 us (0.957)
  Pallas kernels: 112 us -> 108 us
  local copies, waits for them, and re-layouts: 3.12 us -> 1.84 us
    pallas_call x1, Pallas kernels: 112 us -> 108 us  [local(): pl.pallas_call(kernel, name='feti', out_shape=[jax.ShapeDtypeStruct(vec,...]
    unnamed x1 -> x0, local copies, waits for them, and re-layouts: 1.28 us -> none
where the time goes in v3:
time: 112 us
  Pallas kernels  108 us (96%)
  local copies, waits for them, and re-layouts  1.84 us (2%)
  between operations  1.29 us (1%)
    pallas_call x1, Pallas kernels, local(): pl.pallas_call(kernel, name='feti', out_shape=[jax.ShapeDtypeStruct(vec,...  108 us

profile of v3, /device:TPU:1, one launch (start us, length us, event | category | flops | bytes accessed | tf_op | source)
XLA Modules:
  0.0 111.5 jit_solution(933920965921853636)
XLA Ops:
  1.3 108.4 %feti.1 = (f32[20,16,128]{2,1,0:T(8,128)}, f32[20,16,128]{2,1,0:T(8,128)}) custom-call(f32[5,1024,1024]{2,1,0:T(8,128)} %bitcast.17, f32[48,6144]{1,0:T(8,128)} %cinv.1, f32[5,24,1024]{2,1,0:T(8,128)} %bitcast.18, f32[5,4,128]{2,1,0:T(4,128)} %bitcast.22, f32[5,16,4,128]{3,2,1,0:T(4,128)} %bitcast.19, s32[5,4,128]{2,1,0:T(4,128)} %bitcast.23, ...), custom_call_target="tpu_custom_call" | custom-call | tf_op jit(solution)/shard_map/feti/pallas_call | solution.py:644
  109.7 1.8 %copy_bitcast_fusion = (f32[1,1,5,16,4,128]{5,4,3,2,1,0:T(4,128)}, f32[1,1,5,16,4,128]{5,4,3,2,1,0:T(4,128)}) fusion(f32[5,4,16,128]{3,2,1,0:T(8,128)} %bitcast.21, f32[5,4,16,128]{3,2,1,0:T(8,128)} %bitcast.20), kind=kLoop, calls=%fused_computation | loop fusion | bytes 655360 | tf_op jit(solution)/shard_map/broadcast_in_dim | solution.py:668

commit v4 on v3

--- a/solution.py
+++ b/solution.py
@@ -65,6 +65,9 @@
 def group_wait(src, buf, send, recv, peers):
     for i, (device, theirs) in enumerate(peers):
         rcopy(src, buf.at[theirs], send.at[i], recv.at[theirs], device).wait_recv()
+
+
+def group_sent(src, buf, send, recv, peers):
     for i, (device, theirs) in enumerate(peers):
         rcopy(src, buf.at[theirs], send.at[i], recv.at[theirs], device).wait_send()
 
@@ -73,7 +76,7 @@
     flex, cinv, cpl_in, weight_in, rhs_in, dof_in, map_in, partner, counts,
     x_out, r_out,
     stage, flex_hi, flex_lo, m32, m2, cpl, weight, rhs, dof, rowmap, dof_inv, cplp, info, infop,
-    maps_yz, maps_xc, w32, wo, wp, scatter, pick, tbuf, cbuf, xbuf, y1buf, z1buf, y2buf, z2buf,
+    maps_yz, maps_xc, wo, wp, scatter, pick, tbuf, cbuf, xbuf, y1buf, z1buf, y2buf, z2buf,
     psend, precv, qsend, qrecv, gsend, frecv, usend, urecv,
     vblk, vsp, gsp, fsp, yv, tv, dv, sv, zv, rv, mask, ulink, clink, cface, sc,
     pxbuf, pcbuf, pybuf,
@@ -195,15 +198,11 @@
 
     send_maps(info.at[slots], 0)
 
-    w32[...] = jnp.zeros_like(w32)
-
     def build_coupling(source, out):
         for s in range(slots):
-            w32[s, s * corners : (s + 1) * corners, :] = source[s, :, 0:half]
-        for s in range(slots):
-            high, low = split2(w32[s])
-            out[s, 0:width] = high
-            out[s, width:tiles] = low
+            value = source[s, :, 0:half]
+            high = value.astype(BF16).astype(F32)
+            out[s] = jnp.concatenate([high, value - high], axis=0).astype(BF16)
 
     build_coupling(cpl, wo)
     tv[...] = jnp.zeros_like(tv)
@@ -331,8 +330,25 @@
 
         lax.fori_loop(first, last, one, 0)
 
-    def both(value):
-        return value[:, :width] + value[:, width:]
+    def within(s):
+        return jnp.logical_and(lane >= s * corners, lane < (s + 1) * corners)
+
+    def shift(value, by):
+        by = by % width
+        return pltpu.roll(value, by, 1) if by else value
+
+    def sent(it):
+        group_sent(tbuf.at[it, me_yz], tbuf.at[it], t_s.at[it], t_r.at[it], yzs)
+        group_sent(cbuf.at[it, ck], cbuf.at[it], c_s.at[it], c_r.at[it], cs)
+        group_sent(xbuf.at[it, row], xbuf.at[it], x_s.at[it], x_r.at[it], xs)
+        group_sent(y1buf.at[it, cy], y1buf.at[it], y1_s.at[it], y1_r.at[it], ys)
+        group_sent(z1buf.at[it, cz], z1buf.at[it], z1_s.at[it], z1_r.at[it], zs)
+        group_sent(z2buf.at[it, cz], z2buf.at[it], z2_s.at[it], z2_r.at[it], zs)
+        group_sent(y2buf.at[it, cy], y2buf.at[it], y2_s.at[it], y2_r.at[it], ys)
+        rcopy(psend.at[it], precv.at[it], p_s.at[it], p_r.at[it], cs[0][0]).wait_send()
+        group_sent(qsend.at[it, row], qrecv.at[it], q_s.at[it], q_r.at[it], xs)
+        rcopy(gsend.at[it], frecv.at[it], f_s.at[it], f_r.at[it], prev).wait_send()
+        rcopy(usend.at[it], urecv.at[it], u_s.at[it], u_r.at[it], nxt).wait_send()
 
     def body(it, _):
         for b in range(blocks):
@@ -348,11 +364,14 @@
             put3(gsp, p, k, value)
 
         def terms(blocks3, factors):
-            found = None
+            found = jnp.zeros((loads, width), F32)
             for s in range(slots):
-                part = dot(blocks3[s], factors[s], NT)
-                found = part if found is None else found + part
-            return both(sum3(found))
+                part = sum3(dot(blocks3[s], factors[s], NT))
+                rest = jnp.zeros((loads, width - 2 * corners), F32)
+                part = jnp.concatenate([part, rest], axis=1)
+                part = shift(part, s * corners) + shift(part, (s - 1) * corners)
+                found = jnp.where(within(s), part, found)
+            return found
 
         tbuf[it, me_yz, :, 0:width] = terms(vsp, wo)
 
@@ -364,6 +383,10 @@
         tbuf[it, me_yz, :, width:tiles] = terms(gsp, wp)
         group_start(tbuf.at[it, me_yz], tbuf.at[it], me_yz, t_s.at[it], t_r.at[it], yzs)
         tile = scalar_terms(False)
+
+        @pl.when(it > 0)
+        def _():
+            sent(it - 1)
 
         @pl.when(it == 0)
         def _():
@@ -396,8 +419,6 @@
         for copy, (_, q) in reversed(list(zip(arrivals, yzs))):
             copy.wait_recv()
             found = found + spread(q)
-        for copy in arrivals:
-            copy.wait_send()
         cbuf[it, ck, :, 0:rset] = sum3(found)
         cbuf[it, ck, :, rset : rset + width] = tile
         group_start(cbuf.at[it, ck], cbuf.at[it], ck, c_s.at[it], c_r.at[it], cs)
@@ -477,7 +498,7 @@
         core_copy = rcopy(psend.at[it], precv.at[it], p_s.at[it], p_r.at[it], cs[0][0])
         core_copy.start()
         found = sum3(dot(left, pick[ck], NN))
-        core_copy.wait()
+        core_copy.wait_recv()
         for q in range(NX):
             qsend[it, q] = found[:, q * tiles : (q + 1) * tiles] + precv[it, q]
         for i, (d, other) in enumerate(xs):
@@ -497,20 +518,21 @@
                 qsend.at[it, other], qrecv.at[it, other], q_s.at[it, i], q_r.at[it, other], d
             )
             cp.wait_recv()
-            cp.wait_send()
-        picked = stack3(qrecv[it, 0] + qrecv[it, 1] + qrecv[it, 2] + qrecv[it, 3])
-        to_link = jnp.concatenate([picked[:, :width]] * 2, axis=1)
-        to_face = jnp.concatenate([picked[:, width:]] * 2, axis=1)
+        picked = qrecv[it, 0] + qrecv[it, 1] + qrecv[it, 2] + qrecv[it, 3]
+
+        def spread_back(part, s, factors):
+            left = shift(part, -s * corners)
+            left = jnp.where(lane < corners, left, shift(part, (1 - s) * corners))
+            return sum3(dot(stack3(left[:, : 2 * corners]), factors[s], NN))
+
         for s in range(slots):
-            found = sum3(dot(to_link, wo[s], NN))
-            other = sum3(dot(to_face, wp[s], NN))
+            found = spread_back(picked[:, :width], s, wo)
+            other = spread_back(picked[:, width:], s, wp)
             for k in range(links):
                 clink[s * links + k] = found[:, k * width : (k + 1) * width]
                 cface[s * links + k] = other[:, k * width : (k + 1) * width]
 
         answer_copy.wait_recv()
-        answer_copy.wait_send()
-        force_copy.wait_send()
         alpha, beta = sc[2], sc[3]
         for b in range(blocks):
             s, k = b // links, b % links
@@ -525,10 +547,11 @@
 
     lax.fori_loop(0, ITERS, body, 0)
 
+    pxbuf[row] = jnp.sum(scalar_terms(True), axis=0, keepdims=True)
+    group_start(pxbuf.at[row], pxbuf, row, px_s, px_r, xs)
+    sent(ITERS - 1)
     info_copy.wait_send()
     cpl_copy.wait_send()
-    pxbuf[row] = jnp.sum(scalar_terms(True), axis=0, keepdims=True)
-    group_start(pxbuf.at[row], pxbuf, row, px_s, px_r, xs)
     group_wait(pxbuf.at[row], pxbuf, px_s, px_r, xs)
     pcbuf[ck] = pxbuf[0] + pxbuf[1] + pxbuf[2] + pxbuf[3]
     group_start(pcbuf.at[ck], pcbuf, ck, pc_s, pc_r, cs)
@@ -536,6 +559,9 @@
     pybuf[me_yz] = pcbuf[0] + pcbuf[1]
     group_start(pybuf.at[me_yz], pybuf, me_yz, py_s, py_r, yzs)
     group_wait(pybuf.at[me_yz], pybuf, py_s, py_r, yzs)
+    group_sent(pxbuf.at[row], pxbuf, px_s, px_r, xs)
+    group_sent(pcbuf.at[ck], pcbuf, pc_s, pc_r, cs)
+    group_sent(pybuf.at[me_yz], pybuf, py_s, py_r, yzs)
     line = pybuf[0]
     for b in range(1, NYZ):
         line = line + pybuf[b]
@@ -588,9 +614,8 @@
         vm((slots + 1, 1, width), F32),
         vm((NYZ, 2, 1, width), F32),
         vm((nxc, 2, 1, width), F32),
-        vm((slots, width, half), F32),
-        vm((slots, pair, half), BF16),
-        vm((slots, pair, half), BF16),
+        vm((slots, 2 * corners, half), BF16),
+        vm((slots, 2 * corners, half), BF16),
         vm((NYZ, rset, pair), BF16),
         vm((NK, kset, NX * pair), BF16),
         vm(per + (NYZ, loads, pair), F32),

time: 112 us -> 106 us (0.946)
  Pallas kernels: 108 us -> 103 us
    pallas_call x1, Pallas kernels: 108 us -> 103 us  [local(): pl.pallas_call(kernel, name='feti', out_shape=[jax.ShapeDtypeStruct(vec,...]
where the time goes in v4:
time: 106 us
  Pallas kernels  103 us (97%)
  local copies, waits for them, and re-layouts  1.84 us (2%)
  between operations  1.29 us (1%)
    pallas_call x1, Pallas kernels, local(): pl.pallas_call(kernel, name='feti', out_shape=[jax.ShapeDtypeStruct(vec,...  103 us

profile of v4, /device:TPU:1, one launch (start us, length us, event | category | flops | bytes accessed | tf_op | source)
XLA Modules:
  0.0 106.3 jit_solution(166973376813456029)
XLA Ops:
  1.3 103.2 %feti.1 = (f32[20,16,128]{2,1,0:T(8,128)}, f32[20,16,128]{2,1,0:T(8,128)}) custom-call(f32[5,1024,1024]{2,1,0:T(8,128)} %bitcast.17, f32[48,6144]{1,0:T(8,128)} %cinv.1, f32[5,24,1024]{2,1,0:T(8,128)} %bitcast.18, f32[5,4,128]{2,1,0:T(4,128)} %bitcast.22, f32[5,16,4,128]{3,2,1,0:T(4,128)} %bitcast.19, s32[5,4,128]{2,1,0:T(4,128)} %bitcast.23, ...), custom_call_target="tpu_custom_call" | custom-call | tf_op jit(solution)/shard_map/feti/pallas_call | solution.py:669
  104.5 1.8 %copy_bitcast_fusion = (f32[1,1,5,16,4,128]{5,4,3,2,1,0:T(4,128)}, f32[1,1,5,16,4,128]{5,4,3,2,1,0:T(4,128)}) fusion(f32[5,4,16,128]{3,2,1,0:T(8,128)} %bitcast.21, f32[5,4,16,128]{3,2,1,0:T(8,128)} %bitcast.20), kind=kLoop, calls=%fused_computation | loop fusion | bytes 655360 | tf_op jit(solution)/shard_map/broadcast_in_dim | solution.py:693

commit v5 on v4

--- a/solution.py
+++ b/solution.py
@@ -58,18 +58,21 @@
 
 
 def group_start(src, buf, mine, send, recv, peers):
-    for i, (device, _) in enumerate(peers):
-        rcopy(src, buf.at[mine], send.at[i], recv.at[mine], device).start()
-
-
-def group_wait(src, buf, send, recv, peers):
-    for i, (device, theirs) in enumerate(peers):
-        rcopy(src, buf.at[theirs], send.at[i], recv.at[theirs], device).wait_recv()
-
-
-def group_sent(src, buf, send, recv, peers):
-    for i, (device, theirs) in enumerate(peers):
-        rcopy(src, buf.at[theirs], send.at[i], recv.at[theirs], device).wait_send()
+    for device, _ in peers:
+        rcopy(src, buf.at[mine], send, recv, device).start()
+
+
+def group_copy(buf, send, recv, peers):
+    part = buf.at[pl.ds(0, len(peers))]
+    return rcopy(part, part, send, recv, peers[0][0])
+
+
+def group_wait(buf, send, recv, peers):
+    group_copy(buf, send, recv, peers).wait_recv()
+
+
+def group_sent(buf, send, recv, peers):
+    group_copy(buf, send, recv, peers).wait_send()
 
 
 def kernel(
@@ -178,23 +181,20 @@
     loaded[4].wait()
     cpl_copy = rcopy(cpl.at[:, :, half:], cplp, cpl_s, cpl_r, nxt)
     cpl_copy.start()
-    for i, (d, other) in enumerate(xcs):
-        rcopy(m_part(other), m32.at[me_xc], m_s.at[i], m_r.at[me_xc], d).start()
+    for d, other in xcs:
+        rcopy(m_part(other), m32.at[me_xc], m_s, m_r, d).start()
     map_groups = [(maps_yz, me_yz, mapa_s, mapa_r, yzs), (maps_xc, me_xc, mapb_s, mapb_r, xcs)]
 
     def send_maps(src, h):
         for buf, mine, send, recv, peers in map_groups:
-            for i, (d, _) in enumerate(peers):
-                rcopy(src, buf.at[mine, h], send.at[h, i], recv.at[h, mine], d).start()
+            for d, _ in peers:
+                rcopy(src, buf.at[mine, h], send, recv, d).start()
             buf[mine, h] = src[...]
 
-    def wait_maps(h, group):
+    def wait_maps(group):
         buf, _, send, recv, peers = map_groups[group]
-        src = (info, infop)[h].at[slots]
-        for i, (d, other) in enumerate(peers):
-            cp = rcopy(src, buf.at[other, h], send.at[h, i], recv.at[h, other], d)
-            cp.wait_recv()
-            cp.wait_send()
+        group_wait(buf, send, recv, peers)
+        group_sent(buf, send, recv, peers)
 
     send_maps(info.at[slots], 0)
 
@@ -338,15 +338,15 @@
         return pltpu.roll(value, by, 1) if by else value
 
     def sent(it):
-        group_sent(tbuf.at[it, me_yz], tbuf.at[it], t_s.at[it], t_r.at[it], yzs)
-        group_sent(cbuf.at[it, ck], cbuf.at[it], c_s.at[it], c_r.at[it], cs)
-        group_sent(xbuf.at[it, row], xbuf.at[it], x_s.at[it], x_r.at[it], xs)
-        group_sent(y1buf.at[it, cy], y1buf.at[it], y1_s.at[it], y1_r.at[it], ys)
-        group_sent(z1buf.at[it, cz], z1buf.at[it], z1_s.at[it], z1_r.at[it], zs)
-        group_sent(z2buf.at[it, cz], z2buf.at[it], z2_s.at[it], z2_r.at[it], zs)
-        group_sent(y2buf.at[it, cy], y2buf.at[it], y2_s.at[it], y2_r.at[it], ys)
+        group_sent(tbuf.at[it], t_s.at[it], t_r.at[it, 0], yzs)
+        group_sent(cbuf.at[it], c_s.at[it], c_r.at[it], cs)
+        group_sent(xbuf.at[it], x_s.at[it], x_r.at[it], xs)
+        group_sent(y1buf.at[it], y1_s.at[it], y1_r.at[it], ys)
+        group_sent(z1buf.at[it], z1_s.at[it], z1_r.at[it], zs)
+        group_sent(z2buf.at[it], z2_s.at[it], z2_r.at[it], zs)
+        group_sent(y2buf.at[it], y2_s.at[it], y2_r.at[it], ys)
         rcopy(psend.at[it], precv.at[it], p_s.at[it], p_r.at[it], cs[0][0]).wait_send()
-        group_sent(qsend.at[it, row], qrecv.at[it], q_s.at[it], q_r.at[it], xs)
+        group_sent(qrecv.at[it], q_s.at[it], q_r.at[it], xs)
         rcopy(gsend.at[it], frecv.at[it], f_s.at[it], f_r.at[it], prev).wait_send()
         rcopy(usend.at[it], urecv.at[it], u_s.at[it], u_r.at[it], nxt).wait_send()
 
@@ -381,7 +381,10 @@
             build_coupling(cplp, wp)
 
         tbuf[it, me_yz, :, width:tiles] = terms(gsp, wp)
-        group_start(tbuf.at[it, me_yz], tbuf.at[it], me_yz, t_s.at[it], t_r.at[it], yzs)
+        for d, _ in yzs:
+            rcopy(
+                tbuf.at[it, me_yz], tbuf.at[it, me_yz], t_s.at[it], t_r.at[it, me_yz], d
+            ).start()
         tile = scalar_terms(False)
 
         @pl.when(it > 0)
@@ -390,8 +393,7 @@
 
         @pl.when(it == 0)
         def _():
-            wait_maps(0, 0)
-            wait_maps(1, 0)
+            wait_maps(0)
 
             def rows(p, _):
                 base = (lax.rem(p, NX) * cols + me_yz * NK + lax.div(p, NX)) * own_rows
@@ -412,19 +414,15 @@
             return dot(stack3(tbuf[it, q]), scatter[q], NT)
 
         found = spread(me_yz)
-        arrivals = [
-            rcopy(tbuf.at[it, me_yz], tbuf.at[it, q], t_s.at[it, i], t_r.at[it, q], d)
-            for i, (d, q) in enumerate(yzs)
-        ]
-        for copy, (_, q) in reversed(list(zip(arrivals, yzs))):
-            copy.wait_recv()
+        for d, q in reversed(yzs):
+            rcopy(tbuf.at[it, me_yz], tbuf.at[it, q], t_s.at[it], t_r.at[it, q], d).wait_recv()
             found = found + spread(q)
         cbuf[it, ck, :, 0:rset] = sum3(found)
         cbuf[it, ck, :, rset : rset + width] = tile
         group_start(cbuf.at[it, ck], cbuf.at[it], ck, c_s.at[it], c_r.at[it], cs)
         force_copy = rcopy(gsend.at[it], frecv.at[it], f_s.at[it], f_r.at[it], prev)
         force_copy.start()
-        group_wait(cbuf.at[it, ck], cbuf.at[it], c_s.at[it], c_r.at[it], cs)
+        group_wait(cbuf.at[it], c_s.at[it], c_r.at[it], cs)
         xbuf[it, row] = cbuf[it, 0] + cbuf[it, 1]
         group_start(xbuf.at[it, row], xbuf.at[it], row, x_s.at[it], x_r.at[it], xs)
 
@@ -433,16 +431,14 @@
             for s in range(STAGES, slots):
                 convert(s)
             m_local.wait()
-            for i, (d, other) in enumerate(xcs):
-                cp = rcopy(m_part(other), m32.at[other], m_s.at[i], m_r.at[other], d)
-                cp.wait_recv()
-                cp.wait_send()
+            group_wait(m32, m_s, m_r, xcs)
+            group_sent(m32, m_s, m_r, xcs)
             for b in range(nxc):
                 high, low = split2(m32[b])
                 m2[b * own_rows : (b + 1) * own_rows, :] = high
                 m2[rset + b * own_rows : rset + (b + 1) * own_rows, :] = low
 
-        group_wait(xbuf.at[it, row], xbuf.at[it], x_s.at[it], x_r.at[it], xs)
+        group_wait(xbuf.at[it], x_s.at[it], x_r.at[it], xs)
         load = xbuf[it, 0] + xbuf[it, 1] + xbuf[it, 2] + xbuf[it, 3]
         left = stack3(load[:, :rset])
         answer = sum3(dot(jnp.concatenate([left, left], axis=1), m2[...], NN))
@@ -457,8 +453,8 @@
             put3(fsp, b // links, b % links, frecv[it, b])
         local_answers(it, 0, 3)
 
-        group_wait(y1buf.at[it, cy], y1buf.at[it], y1_s.at[it], y1_r.at[it], ys)
-        group_wait(z1buf.at[it, cz], z1buf.at[it], z1_s.at[it], z1_r.at[it], zs)
+        group_wait(y1buf.at[it], y1_s.at[it], y1_r.at[it], ys)
+        group_wait(z1buf.at[it], z1_s.at[it], z1_r.at[it], zs)
         z2buf[it, cz] = y1buf[it, 0] + y1buf[it, 1] + y1buf[it, 2] + y1buf[it, 3]
         y2buf[it, cy] = z1buf[it, 0] + z1buf[it, 1] + z1buf[it, 2] + z1buf[it, 3]
         group_start(z2buf.at[it, cz], z2buf.at[it], cz, z2_s.at[it], z2_r.at[it], zs)
@@ -467,8 +463,7 @@
 
         @pl.when(it == 0)
         def _():
-            wait_maps(0, 1)
-            wait_maps(1, 1)
+            wait_maps(1)
             step = own_rows
 
             def rows(b, _):
@@ -484,8 +479,8 @@
 
             lax.fori_loop(0, kset // step, rows, 0)
 
-        group_wait(z2buf.at[it, cz], z2buf.at[it], z2_s.at[it], z2_r.at[it], zs)
-        group_wait(y2buf.at[it, cy], y2buf.at[it], y2_s.at[it], y2_r.at[it], ys)
+        group_wait(z2buf.at[it], z2_s.at[it], z2_r.at[it], zs)
+        group_wait(y2buf.at[it], y2_s.at[it], y2_r.at[it], ys)
         answer_copy = rcopy(usend.at[it], urecv.at[it], u_s.at[it], u_r.at[it], nxt)
         answer_copy.start()
         first = z2buf[it, 0] + z2buf[it, 1] + z2buf[it, 2] + z2buf[it, 3]
@@ -501,10 +496,8 @@
         core_copy.wait_recv()
         for q in range(NX):
             qsend[it, q] = found[:, q * tiles : (q + 1) * tiles] + precv[it, q]
-        for i, (d, other) in enumerate(xs):
-            rcopy(
-                qsend.at[it, other], qrecv.at[it, row], q_s.at[it, i], q_r.at[it, row], d
-            ).start()
+        for d, other in xs:
+            rcopy(qsend.at[it, other], qrecv.at[it, row], q_s.at[it], q_r.at[it], d).start()
         qrecv[it, row] = qsend[it, row]
 
         @pl.when(it > 0)
@@ -513,11 +506,7 @@
             for b in range(blocks):
                 zv[b] = weight_of(b) * resid[b]
 
-        for i, (d, other) in enumerate(xs):
-            cp = rcopy(
-                qsend.at[it, other], qrecv.at[it, other], q_s.at[it, i], q_r.at[it, other], d
-            )
-            cp.wait_recv()
+        group_wait(qrecv.at[it], q_s.at[it], q_r.at[it], xs)
         picked = qrecv[it, 0] + qrecv[it, 1] + qrecv[it, 2] + qrecv[it, 3]
 
         def spread_back(part, s, factors):
@@ -552,16 +541,16 @@
     sent(ITERS - 1)
     info_copy.wait_send()
     cpl_copy.wait_send()
-    group_wait(pxbuf.at[row], pxbuf, px_s, px_r, xs)
+    group_wait(pxbuf, px_s, px_r, xs)
     pcbuf[ck] = pxbuf[0] + pxbuf[1] + pxbuf[2] + pxbuf[3]
     group_start(pcbuf.at[ck], pcbuf, ck, pc_s, pc_r, cs)
-    group_wait(pcbuf.at[ck], pcbuf, pc_s, pc_r, cs)
+    group_wait(pcbuf, pc_s, pc_r, cs)
     pybuf[me_yz] = pcbuf[0] + pcbuf[1]
     group_start(pybuf.at[me_yz], pybuf, me_yz, py_s, py_r, yzs)
-    group_wait(pybuf.at[me_yz], pybuf, py_s, py_r, yzs)
-    group_sent(pxbuf.at[row], pxbuf, px_s, px_r, xs)
-    group_sent(pcbuf.at[ck], pcbuf, pc_s, pc_r, cs)
-    group_sent(pybuf.at[me_yz], pybuf, py_s, py_r, yzs)
+    group_wait(pybuf, py_s, py_r, yzs)
+    group_sent(pxbuf, px_s, px_r, xs)
+    group_sent(pcbuf, pc_s, pc_r, cs)
+    group_sent(pybuf, py_s, py_r, yzs)
     line = pybuf[0]
     for b in range(1, NYZ):
         line = line + pybuf[b]
@@ -651,18 +640,16 @@
         dma,
         dma,
         dma,
-        dma((2, NYZ - 1)),
-        dma((2, NYZ)),
-        dma((2, nxc - 1)),
-        dma((2, nxc)),
-        dma((nxc - 1,)),
-        dma((nxc,)),
+        dma,
+        dma,
+        dma,
+        dma,
+        dma,
+        dma,
+        dma(per),
+        dma(per + (NYZ,)),
     ]
-    for size in (NYZ, NK, NX, NY, NZ, NY, NZ):
-        scratch += [dma(per + (size - 1,)), dma(per + (size,))]
-    scratch += [dma(per)] * 2 + [dma(per + (NX - 1,)), dma(per + (NX,))] + [dma(per)] * 4
-    for size in (NX, NK, NYZ):
-        scratch += [dma((size - 1,)), dma((size,))]
+    scratch += [dma(per)] * 20 + [dma] * 6
     in_vmem = pl.BlockSpec(memory_space=pltpu.VMEM)
     in_smem = pl.BlockSpec(memory_space=pltpu.SMEM)
     in_place = pl.BlockSpec(memory_space=pl.ANY)

time: 106 us -> 104 us (0.981)
  Pallas kernels: 103 us -> 101 us
    pallas_call x1, Pallas kernels: 103 us -> 101 us  [local(): pl.pallas_call(kernel, name='feti', out_shape=[jax.ShapeDtypeStruct(vec,...]
where the time goes in v5:
time: 104 us
  Pallas kernels  101 us (97%)
  local copies, waits for them, and re-layouts  1.84 us (2%)
  between operations  1.29 us (1%)
    pallas_call x1, Pallas kernels, local(): pl.pallas_call(kernel, name='feti', out_shape=[jax.ShapeDtypeStruct(vec,...  101 us

profile of v5, /device:TPU:1, one launch (start us, length us, event | category | flops | bytes accessed | tf_op | source)
XLA Modules:
  0.0 103.8 jit_solution(15556044929421113322)
XLA Ops:
  1.3 100.6 %feti.1 = (f32[20,16,128]{2,1,0:T(8,128)}, f32[20,16,128]{2,1,0:T(8,128)}) custom-call(f32[5,1024,1024]{2,1,0:T(8,128)} %bitcast.17, f32[48,6144]{1,0:T(8,128)} %cinv.1, f32[5,24,1024]{2,1,0:T(8,128)} %bitcast.18, f32[5,4,128]{2,1,0:T(4,128)} %bitcast.22, f32[5,16,4,128]{3,2,1,0:T(4,128)} %bitcast.19, s32[5,4,128]{2,1,0:T(4,128)} %bitcast.23, ...), custom_call_target="tpu_custom_call" | custom-call | tf_op jit(solution)/shard_map/feti/pallas_call | solution.py:656
  101.9 1.8 %copy_bitcast_fusion = (f32[1,1,5,16,4,128]{5,4,3,2,1,0:T(4,128)}, f32[1,1,5,16,4,128]{5,4,3,2,1,0:T(4,128)}) fusion(f32[5,4,16,128]{3,2,1,0:T(8,128)} %bitcast.21, f32[5,4,16,128]{3,2,1,0:T(8,128)} %bitcast.20), kind=kLoop, calls=%fused_computation | loop fusion | bytes 655360 | tf_op jit(solution)/shard_map/broadcast_in_dim | solution.py:680

commit v6 on v5

--- a/solution.py
+++ b/solution.py
@@ -82,10 +82,10 @@
     maps_yz, maps_xc, wo, wp, scatter, pick, tbuf, cbuf, xbuf, y1buf, z1buf, y2buf, z2buf,
     psend, precv, qsend, qrecv, gsend, frecv, usend, urecv,
     vblk, vsp, gsp, fsp, yv, tv, dv, sv, zv, rv, mask, ulink, clink, cface, sc,
-    pxbuf, pcbuf, pybuf,
+    pybuf,
     flex_sem, load_sem, mloc_sem, info_s, info_r, cpl_s, cpl_r, mapa_s, mapa_r, mapb_s, mapb_r,
     m_s, m_r, t_s, t_r, c_s, c_r, x_s, x_r, y1_s, y1_r, z1_s, z1_r, y2_s, y2_r, z2_s, z2_r,
-    p_s, p_r, q_s, q_r, f_s, f_r, u_s, u_r, px_s, px_r, pc_s, pc_r, py_s, py_r,
+    p_s, p_r, q_s, q_r, f_s, f_r, u_s, u_r, py_s, py_r,
 ):
     slots, iface = flex.shape[:2]
     half = iface // 2
@@ -536,24 +536,23 @@
 
     lax.fori_loop(0, ITERS, body, 0)
 
-    pxbuf[row] = jnp.sum(scalar_terms(True), axis=0, keepdims=True)
-    group_start(pxbuf.at[row], pxbuf, row, px_s, px_r, xs)
+    me_all = row * cols + col
+    pybuf[me_all] = jnp.sum(scalar_terms(True), axis=0, keepdims=True)
+
+    def tell(i, _):
+        d = (turn(row, lax.div(i, cols), NX), turn(col, lax.rem(i, cols), cols))
+        rcopy(pybuf.at[me_all], pybuf.at[me_all], py_s, py_r, d).start()
+        return 0
+
+    lax.fori_loop(1, NX * cols, tell, 0)
     sent(ITERS - 1)
     info_copy.wait_send()
     cpl_copy.wait_send()
-    group_wait(pxbuf, px_s, px_r, xs)
-    pcbuf[ck] = pxbuf[0] + pxbuf[1] + pxbuf[2] + pxbuf[3]
-    group_start(pcbuf.at[ck], pcbuf, ck, pc_s, pc_r, cs)
-    group_wait(pcbuf, pc_s, pc_r, cs)
-    pybuf[me_yz] = pcbuf[0] + pcbuf[1]
-    group_start(pybuf.at[me_yz], pybuf, me_yz, py_s, py_r, yzs)
-    group_wait(pybuf, py_s, py_r, yzs)
-    group_sent(pxbuf, px_s, px_r, xs)
-    group_sent(pcbuf, pc_s, pc_r, cs)
-    group_sent(pybuf, py_s, py_r, yzs)
-    line = pybuf[0]
-    for b in range(1, NYZ):
-        line = line + pybuf[b]
+    everything = pybuf.at[pl.ds(0, NX * cols - 1)]
+    final = rcopy(everything, everything, py_s, py_r, nxt)
+    final.wait_recv()
+    line = jnp.sum(pybuf[...], axis=0)
+    final.wait_send()
     r_out[...] = update(jnp.broadcast_to(line, (loads, width)), True, None)
 
 
@@ -630,9 +629,7 @@
     scratch += [vm(vec, F32)] * 10
     scratch += [
         vm((4, loads, width), F32),
-        vm((NX, 1, width), F32),
-        vm((NK, 1, width), F32),
-        vm((NYZ, 1, width), F32),
+        vm((NYZ * nxc, 1, width), F32),
         dma((slots,)),
         dma((5,)),
         dma,
@@ -649,7 +646,7 @@
         dma(per),
         dma(per + (NYZ,)),
     ]
-    scratch += [dma(per)] * 20 + [dma] * 6
+    scratch += [dma(per)] * 20 + [dma] * 2
     in_vmem = pl.BlockSpec(memory_space=pltpu.VMEM)
     in_smem = pl.BlockSpec(memory_space=pltpu.SMEM)
     in_place = pl.BlockSpec(memory_space=pl.ANY)

time: 104 us -> 103 us (level)
  Pallas kernels: 101 us -> 99.4 us
    pallas_call x1, Pallas kernels: 101 us -> 99.4 us  [local(): pl.pallas_call(kernel, name='feti', out_shape=[jax.ShapeDtypeStruct(vec,...]
where the time goes in v6:
time: 103 us
  Pallas kernels  99.4 us (97%)
  local copies, waits for them, and re-layouts  1.84 us (2%)
  between operations  1.29 us (1%)
    pallas_call x1, Pallas kernels, local(): pl.pallas_call(kernel, name='feti', out_shape=[jax.ShapeDtypeStruct(vec,...  99.4 us

profile of v6, /device:TPU:1, one launch (start us, length us, event | category | flops | bytes accessed | tf_op | source)
XLA Modules:
  0.0 102.5 jit_solution(6912743518792266024)
XLA Ops:
  1.3 99.4 %feti.1 = (f32[20,16,128]{2,1,0:T(8,128)}, f32[20,16,128]{2,1,0:T(8,128)}) custom-call(f32[5,1024,1024]{2,1,0:T(8,128)} %bitcast.17, f32[48,6144]{1,0:T(8,128)} %cinv.1, f32[5,24,1024]{2,1,0:T(8,128)} %bitcast.18, f32[5,4,128]{2,1,0:T(4,128)} %bitcast.22, f32[5,16,4,128]{3,2,1,0:T(4,128)} %bitcast.19, s32[5,4,128]{2,1,0:T(4,128)} %bitcast.23, ...), custom_call_target="tpu_custom_call" | custom-call | tf_op jit(solution)/shard_map/feti/pallas_call | solution.py:653
  100.7 1.8 %copy_bitcast_fusion = (f32[1,1,5,16,4,128]{5,4,3,2,1,0:T(4,128)}, f32[1,1,5,16,4,128]{5,4,3,2,1,0:T(4,128)}) fusion(f32[5,4,16,128]{3,2,1,0:T(8,128)} %bitcast.21, f32[5,4,16,128]{3,2,1,0:T(8,128)} %bitcast.20), kind=kLoop, calls=%fused_computation | loop fusion | bytes 655360 | tf_op jit(solution)/shard_map/broadcast_in_dim | solution.py:677

commit v7 on v6

--- a/solution.py
+++ b/solution.py
@@ -27,10 +27,7 @@
 
 def split3(value):
     high = value.astype(BF16)
-    rest = value - high.astype(F32)
-    middle = rest.astype(BF16)
-    low = (rest - middle.astype(F32)).astype(BF16)
-    return high, middle, low
+    return high, (value - high.astype(F32)).astype(BF16)
 
 
 def stack3(value):
@@ -42,8 +39,8 @@
 
 
 def sum3(value):
-    rows = value.shape[0] // 3
-    return value[2 * rows :] + value[rows : 2 * rows] + value[:rows]
+    rows = value.shape[0] // 2
+    return value[rows:] + value[:rows]
 
 
 def rcopy(src, dst, send, recv, device):
@@ -99,6 +96,7 @@
     khalf = kset // 2
     blocks = slots * links
     tiles = 2 * width
+    spare = slots * corners
 
     row, col = lax.axis_index("row"), lax.axis_index("col")
     cz = lax.div(col, NY * NK)
@@ -235,6 +233,14 @@
     info_copy.wait_recv()
     send_maps(infop.at[slots], 1)
 
+    def put3(ref, s, k, value):
+        for i, part in enumerate(split3(value)):
+            ref[s, i * loads : (i + 1) * loads, k * width : (k + 1) * width] = part
+
+    def multipliers(b, value):
+        vblk[b] = value
+        put3(vsp, b // links, b % links, value)
+
     def weight_of(b):
         return weight[b // links, b % links : b % links + 1, :]
 
@@ -246,7 +252,9 @@
         resid = live * rhs[s, :, k, :]
         rv[b] = resid
         yv[b] = resid
-        zv[b] = weight_of(b) * resid
+        value = weight_of(b) * resid
+        zv[b] = value
+        multipliers(b, value)
 
     lane = lax.broadcasted_iota(jnp.int32, (loads, width), 1)
     load_id = lax.broadcasted_iota(jnp.int32, (loads, width), 0)
@@ -259,7 +267,7 @@
         found = [total(rv[...], z), total(z, y), total(z, sv[...]), total(dv[...], y)]
         tile = jnp.zeros((loads, width), F32)
         for i, value in enumerate(found):
-            at = lane == (4 * load_id + i if packed else i)
+            at = lane == (4 * load_id + i if packed else spare + i)
             tile = jnp.where(at, value, tile)
         return tile
 
@@ -267,7 +275,7 @@
         rz, zy, zs_, dy = [
             jnp.broadcast_to(
                 jnp.sum(
-                    jnp.where(lane == (4 * load_id + i if packed else i), tile, 0.0),
+                    jnp.where(lane == (4 * load_id + i if packed else spare + i), tile, 0.0),
                     axis=1,
                     keepdims=True,
                 ),
@@ -290,10 +298,6 @@
         rv[...] = resid
         return resid
 
-    def put3(ref, s, k, value):
-        for i, part in enumerate(split3(value)):
-            ref[s, i * loads : (i + 1) * loads, k * width : (k + 1) * width] = part
-
     def take(value, index):
         return jnp.take_along_axis(value, index, axis=1, mode="promise_in_bounds")
 
@@ -352,10 +356,6 @@
 
     def body(it, _):
         for b in range(blocks):
-            value = weight_of(b) * yv[b]
-            vblk[b] = value
-            put3(vsp, b // links, b % links, value)
-        for b in range(blocks):
             p, k = b // links, b % links
             from_block = inverse[k, p] * links + k
             index = jnp.concatenate([dof_inv[from_block]] * (loads // 8), axis=0)
@@ -373,7 +373,9 @@
                 found = jnp.where(within(s), part, found)
             return found
 
-        tbuf[it, me_yz, :, 0:width] = terms(vsp, wo)
+        tbuf[it, me_yz, :, 0:width] = jnp.where(
+            lane < spare, terms(vsp, wo), scalar_terms(False)
+        )
 
         @pl.when(it == 0)
         def _():
@@ -385,8 +387,6 @@
             rcopy(
                 tbuf.at[it, me_yz], tbuf.at[it, me_yz], t_s.at[it], t_r.at[it, me_yz], d
             ).start()
-        tile = scalar_terms(False)
-
         @pl.when(it > 0)
         def _():
             sent(it - 1)
@@ -413,12 +413,12 @@
         def spread(q):
             return dot(stack3(tbuf[it, q]), scatter[q], NT)
 
-        found = spread(me_yz)
+        found, carried = spread(me_yz), tbuf[it, me_yz, :, 0:width]
         for d, q in reversed(yzs):
             rcopy(tbuf.at[it, me_yz], tbuf.at[it, q], t_s.at[it], t_r.at[it, q], d).wait_recv()
-            found = found + spread(q)
+            found, carried = found + spread(q), carried + tbuf[it, q, :, 0:width]
         cbuf[it, ck, :, 0:rset] = sum3(found)
-        cbuf[it, ck, :, rset : rset + width] = tile
+        cbuf[it, ck, :, rset : rset + width] = carried
         group_start(cbuf.at[it, ck], cbuf.at[it], ck, c_s.at[it], c_r.at[it], cs)
         force_copy = rcopy(gsend.at[it], frecv.at[it], f_s.at[it], f_r.at[it], prev)
         force_copy.start()
@@ -442,8 +442,7 @@
         load = xbuf[it, 0] + xbuf[it, 1] + xbuf[it, 2] + xbuf[it, 3]
         left = stack3(load[:, :rset])
         answer = sum3(dot(jnp.concatenate([left, left], axis=1), m2[...], NN))
-        y1buf[it, cy, :, 0:khalf] = answer[:, :khalf]
-        y1buf[it, cy, :, khalf : khalf + width] = load[:, rset:]
+        y1buf[it, cy] = answer[:, :khalf]
         z1buf[it, cz] = answer[:, khalf:]
         group_start(y1buf.at[it, cy], y1buf.at[it], cy, y1_s.at[it], y1_r.at[it], ys)
         group_start(z1buf.at[it, cz], z1buf.at[it], cz, z1_s.at[it], z1_r.at[it], zs)
@@ -485,8 +484,7 @@
         answer_copy.start()
         first = z2buf[it, 0] + z2buf[it, 1] + z2buf[it, 2] + z2buf[it, 3]
         second = y2buf[it, 0] + y2buf[it, 1] + y2buf[it, 2] + y2buf[it, 3]
-        scalars = first[:, khalf:]
-        left = stack3(jnp.concatenate([first[:, :khalf], second], axis=1))
+        left = stack3(jnp.concatenate([first, second], axis=1))
         found = sum3(dot(left, pick[1 - ck], NN))
         for q in range(NX):
             psend[it, q] = found[:, q * tiles : (q + 1) * tiles]
@@ -502,7 +500,7 @@
 
         @pl.when(it > 0)
         def _():
-            resid = update(scalars, False, it == 1)
+            resid = update(load[:, rset:], False, it == 1)
             for b in range(blocks):
                 zv[b] = weight_of(b) * resid[b]
 
@@ -531,7 +529,9 @@
             image = (ulink[b] + clink[b] - far) * mask[b]
             image = image + beta * tv[b]
             tv[b] = jnp.where(it == 0, 0.0, image)
-            yv[b] = jnp.where(it == 0, image, yv[b] - alpha * image)
+            image = jnp.where(it == 0, image, yv[b] - alpha * image)
+            yv[b] = image
+            multipliers(b, weight_of(b) * image)
         return 0
 
     lax.fori_loop(0, ITERS, body, 0)
@@ -578,7 +578,7 @@
     blocks = slots * links
     nxc = NX * NK
     kset, rset = coarse // nxc, own_rows * nxc
-    rows3 = 3 * loads
+    rows3 = 2 * loads
     pair = 2 * width
 
     vec = (blocks, loads, width)
@@ -609,10 +609,10 @@
         vm(per + (NYZ, loads, pair), F32),
         vm(per + (NK, loads, rset + width), F32),
         vm(per + (NX, loads, rset + width), F32),
-        vm(per + (NY, loads, kset // 2 + width), F32),
+        vm(per + (NY, loads, kset // 2), F32),
         vm(per + (NZ, loads, kset // 2), F32),
         vm(per + (NY, loads, kset // 2), F32),
-        vm(per + (NZ, loads, kset // 2 + width), F32),
+        vm(per + (NZ, loads, kset // 2), F32),
         vm(per + (NX, loads, pair), F32),
         vm(per + (NX, loads, pair), F32),
         vm(per + (NX, loads, pair), F32),

time: 103 us -> 101 us (0.981)
  Pallas kernels: 99.4 us -> 97.8 us
    pallas_call x1, Pallas kernels: 99.4 us -> 97.8 us  [local(): pl.pallas_call(kernel, name='feti', out_shape=[jax.ShapeDtypeStruct(vec,...]
where the time goes in v7:
time: 101 us
  Pallas kernels  97.8 us (97%)
  local copies, waits for them, and re-layouts  1.84 us (2%)
  between operations  1.29 us (1%)
    pallas_call x1, Pallas kernels, local(): pl.pallas_call(kernel, name='feti', out_shape=[jax.ShapeDtypeStruct(vec,...  97.8 us

profile of v7, /device:TPU:1, one launch (start us, length us, event | category | flops | bytes accessed | tf_op | source)
XLA Modules:
  0.0 100.9 jit_solution(5994887278650709946)
XLA Ops:
  1.3 97.8 %feti.1 = (f32[20,16,128]{2,1,0:T(8,128)}, f32[20,16,128]{2,1,0:T(8,128)}) custom-call(f32[5,1024,1024]{2,1,0:T(8,128)} %bitcast.17, f32[48,6144]{1,0:T(8,128)} %cinv.1, f32[5,24,1024]{2,1,0:T(8,128)} %bitcast.18, f32[5,4,128]{2,1,0:T(4,128)} %bitcast.22, f32[5,16,4,128]{3,2,1,0:T(4,128)} %bitcast.19, s32[5,4,128]{2,1,0:T(4,128)} %bitcast.23, ...), custom_call_target="tpu_custom_call" | custom-call | tf_op jit(solution)/shard_map/feti/pallas_call | solution.py:653
  99.1 1.8 %copy_bitcast_fusion = (f32[1,1,5,16,4,128]{5,4,3,2,1,0:T(4,128)}, f32[1,1,5,16,4,128]{5,4,3,2,1,0:T(4,128)}) fusion(f32[5,4,16,128]{3,2,1,0:T(8,128)} %bitcast.21, f32[5,4,16,128]{3,2,1,0:T(8,128)} %bitcast.20), kind=kLoop, calls=%fused_computation | loop fusion | bytes 655360 | tf_op jit(solution)/shard_map/broadcast_in_dim | solution.py:677

commit v8 on v7

--- a/solution.py
+++ b/solution.py
@@ -80,7 +80,8 @@
     psend, precv, qsend, qrecv, gsend, frecv, usend, urecv,
     vblk, vsp, gsp, fsp, yv, tv, dv, sv, zv, rv, mask, ulink, clink, cface, sc,
     pybuf,
-    flex_sem, load_sem, mloc_sem, info_s, info_r, cpl_s, cpl_r, mapa_s, mapa_r, mapb_s, mapb_r,
+    flex_sem, load_sem, mloc_sem, info_s, info_r, cpl_s, cpl_r, mapn_s, mapn_r, mapa_s, mapa_r,
+    mapb_s, mapb_r,
     m_s, m_r, t_s, t_r, c_s, c_r, x_s, x_r, y1_s, y1_r, z1_s, z1_r, y2_s, y2_r, z2_s, z2_r,
     p_s, p_r, q_s, q_r, f_s, f_r, u_s, u_r, py_s, py_r,
 ):
@@ -133,8 +134,10 @@
         if (i, j) != (0, 0)
     ]
 
+    near = [p for p, (i, j) in zip(yzs, order) if i == 0 or j == 0]
+    far = [p for p, (i, j) in zip(yzs, order) if i != 0 and j != 0]
     barrier = pltpu.get_barrier_semaphore()
-    everyone = [d for d, _ in yzs] + [d for d, _ in xcs] + [prev, nxt]
+    everyone = [d for d, _ in near] + [d for d, _ in xcs] + [prev, nxt]
     for d in everyone:
         pl.semaphore_signal(barrier, inc=1, device_id=d, device_id_type=MESH)
 
@@ -181,20 +184,15 @@
     cpl_copy.start()
     for d, other in xcs:
         rcopy(m_part(other), m32.at[me_xc], m_s, m_r, d).start()
-    map_groups = [(maps_yz, me_yz, mapa_s, mapa_r, yzs), (maps_xc, me_xc, mapb_s, mapb_r, xcs)]
-
-    def send_maps(src, h):
-        for buf, mine, send, recv, peers in map_groups:
-            for d, _ in peers:
-                rcopy(src, buf.at[mine, h], send, recv, d).start()
-            buf[mine, h] = src[...]
-
-    def wait_maps(group):
-        buf, _, send, recv, peers = map_groups[group]
-        group_wait(buf, send, recv, peers)
-        group_sent(buf, send, recv, peers)
-
-    send_maps(info.at[slots], 0)
+    def send_maps(src, h, buf, mine, send, recv, peers):
+        for d, _ in peers:
+            rcopy(src, buf.at[mine, h], send, recv, d).start()
+
+    own_map, prev_map = info.at[slots], infop.at[slots]
+    send_maps(own_map, 0, maps_yz, me_yz, mapn_s, mapn_r, near)
+    send_maps(own_map, 0, maps_xc, me_xc, mapb_s, mapb_r, xcs)
+    maps_yz[me_yz, 0] = info[slots]
+    maps_xc[me_xc, 0] = info[slots]
 
     def build_coupling(source, out):
         for s in range(slots):
@@ -231,7 +229,14 @@
     loaded[2].wait()
     loaded[3].wait()
     info_copy.wait_recv()
-    send_maps(infop.at[slots], 1)
+    near_maps = maps_yz.at[pl.ds(0, len(near)), 0]
+    near_copy = rcopy(near_maps, near_maps, mapn_s, mapn_r, near[0][0])
+    near_copy.wait_recv()
+    send_maps(prev_map, 1, maps_yz, me_yz, mapa_s, mapa_r, yzs)
+    send_maps(own_map, 0, maps_yz, me_yz, mapa_s, mapa_r, far)
+    send_maps(prev_map, 1, maps_xc, me_xc, mapb_s, mapb_r, xcs)
+    maps_yz[me_yz, 1] = infop[slots]
+    maps_xc[me_xc, 1] = infop[slots]
 
     def put3(ref, s, k, value):
         for i, part in enumerate(split3(value)):
@@ -393,7 +398,11 @@
 
         @pl.when(it == 0)
         def _():
-            wait_maps(0)
+            late = maps_yz.at[pl.ds(0, (len(yzs) + len(far)) // 2)]
+            late_copy = rcopy(late, late, mapa_s, mapa_r, near[0][0])
+            late_copy.wait_recv()
+            late_copy.wait_send()
+            near_copy.wait_send()
 
             def rows(p, _):
                 base = (lax.rem(p, NX) * cols + me_yz * NK + lax.div(p, NX)) * own_rows
@@ -462,7 +471,8 @@
 
         @pl.when(it == 0)
         def _():
-            wait_maps(1)
+            group_wait(maps_xc, mapb_s, mapb_r, xcs)
+            group_sent(maps_xc, mapb_s, mapb_r, xcs)
             step = own_rows
 
             def rows(b, _):
@@ -525,8 +535,8 @@
             s, k = b // links, b % links
             facing = partner[k, s] * links + k
             index = jnp.broadcast_to(dof[s, k : k + 1, :], (loads, width))
-            far = take(urecv[it, facing] + cface[facing], index)
-            image = (ulink[b] + clink[b] - far) * mask[b]
+            faced = take(urecv[it, facing] + cface[facing], index)
+            image = (ulink[b] + clink[b] - faced) * mask[b]
             image = image + beta * tv[b]
             tv[b] = jnp.where(it == 0, 0.0, image)
             image = jnp.where(it == 0, image, yv[b] - alpha * image)
@@ -643,6 +653,8 @@
         dma,
         dma,
         dma,
+        dma,
+        dma,
         dma(per),
         dma(per + (NYZ,)),
     ]

time: 101 us -> 103 us (1.020)
  Pallas kernels: 97.8 us -> 99.3 us
    pallas_call x1, Pallas kernels: 97.8 us -> 99.3 us  [local(): pl.pallas_call(kernel, name='feti', out_shape=[jax.ShapeDtypeStruct(vec,...]
where the time goes in v8:
time: 103 us; the launch traced here: 102 us
  Pallas kernels  99.3 us (96%)
  local copies, waits for them, and re-layouts  1.84 us (2%)
  between operations  1.29 us (1%)
    pallas_call x1, Pallas kernels, local(): pl.pallas_call(kernel, name='feti', out_shape=[jax.ShapeDtypeStruct(vec,...  99.3 us

profile of v8, /device:TPU:1, one launch (start us, length us, event | category | flops | bytes accessed | tf_op | source)
XLA Modules:
  0.0 102.5 jit_solution(7059032432102860346)
XLA Ops:
  1.3 99.3 %feti.1 = (f32[20,16,128]{2,1,0:T(8,128)}, f32[20,16,128]{2,1,0:T(8,128)}) custom-call(f32[5,1024,1024]{2,1,0:T(8,128)} %bitcast.17, f32[48,6144]{1,0:T(8,128)} %cinv.1, f32[5,24,1024]{2,1,0:T(8,128)} %bitcast.18, f32[5,4,128]{2,1,0:T(4,128)} %bitcast.22, f32[5,16,4,128]{3,2,1,0:T(4,128)} %bitcast.19, s32[5,4,128]{2,1,0:T(4,128)} %bitcast.23, ...), custom_call_target="tpu_custom_call" | custom-call | tf_op jit(solution)/shard_map/feti/pallas_call | solution.py:665
  100.6 1.8 %copy_bitcast_fusion = (f32[1,1,5,16,4,128]{5,4,3,2,1,0:T(4,128)}, f32[1,1,5,16,4,128]{5,4,3,2,1,0:T(4,128)}) fusion(f32[5,4,16,128]{3,2,1,0:T(8,128)} %bitcast.21, f32[5,4,16,128]{3,2,1,0:T(8,128)} %bitcast.20), kind=kLoop, calls=%fused_computation | loop fusion | bytes 655360 | tf_op jit(solution)/shard_map/broadcast_in_dim | solution.py:689

commit v9 on v7

--- a/solution.py
+++ b/solution.py
@@ -539,12 +539,23 @@
     me_all = row * cols + col
     pybuf[me_all] = jnp.sum(scalar_terms(True), axis=0, keepdims=True)
 
-    def tell(i, _):
-        d = (turn(row, lax.div(i, cols), NX), turn(col, lax.rem(i, cols), cols))
-        rcopy(pybuf.at[me_all], pybuf.at[me_all], py_s, py_r, d).start()
-        return 0
-
-    lax.fori_loop(1, NX * cols, tell, 0)
+    group = 8
+
+    def tell(x, first):
+        def some(n, _):
+            for j in range(group):
+                d = (x, lax.rem(col + n * group + j, cols))
+                rcopy(pybuf.at[me_all], pybuf.at[me_all], py_s, py_r, d).start()
+            return 0
+
+        for j in range(first, group if first else 0):
+            d = (x, lax.rem(col + j, cols))
+            rcopy(pybuf.at[me_all], pybuf.at[me_all], py_s, py_r, d).start()
+        lax.fori_loop(1 if first else 0, cols // group, some, 0)
+
+    for i in (2, 1, 3):
+        tell(turn(row, i, NX), 0)
+    tell(row, 1)
     sent(ITERS - 1)
     info_copy.wait_send()
     cpl_copy.wait_send()

time: 101 us -> 100 us (0.990)
  no operation moved by 1% of the time
where the time goes in v9:
time: 100 us
  Pallas kernels  97 us (97%)
  local copies, waits for them, and re-layouts  1.84 us (2%)
  between operations  1.29 us (1%)
    pallas_call x1, Pallas kernels, local(): pl.pallas_call(kernel, name='feti', out_shape=[jax.ShapeDtypeStruct(vec,...  97 us

profile of v9, /device:TPU:1, one launch (start us, length us, event | category | flops | bytes accessed | tf_op | source)
XLA Modules:
  0.0 100.1 jit_solution(14663289241807170222)
XLA Ops:
  1.3 97.0 %feti.1 = (f32[20,16,128]{2,1,0:T(8,128)}, f32[20,16,128]{2,1,0:T(8,128)}) custom-call(f32[5,1024,1024]{2,1,0:T(8,128)} %bitcast.17, f32[48,6144]{1,0:T(8,128)} %cinv.1, f32[5,24,1024]{2,1,0:T(8,128)} %bitcast.18, f32[5,4,128]{2,1,0:T(4,128)} %bitcast.22, f32[5,16,4,128]{3,2,1,0:T(4,128)} %bitcast.19, s32[5,4,128]{2,1,0:T(4,128)} %bitcast.23, ...), custom_call_target="tpu_custom_call" | custom-call | tf_op jit(solution)/shard_map/feti/pallas_call | solution.py:664
  98.3 1.8 %copy_bitcast_fusion = (f32[1,1,5,16,4,128]{5,4,3,2,1,0:T(4,128)}, f32[1,1,5,16,4,128]{5,4,3,2,1,0:T(4,128)}) fusion(f32[5,4,16,128]{3,2,1,0:T(8,128)} %bitcast.21, f32[5,4,16,128]{3,2,1,0:T(8,128)} %bitcast.20), kind=kLoop, calls=%fused_computation | loop fusion | bytes 655360 | tf_op jit(solution)/shard_map/broadcast_in_dim | solution.py:688
